TPU v7x, 512 devices: a whole 4x4x16 slice. The times are simulated.
512 devices in a mesh: load: 16 (over x, y), gx: 8 (over z_lo, core), gy: 4 (over z_hi).
Axes of the slice: x: 4, y: 4, z: 16 (z_hi: 4, z_lo: 4; z = z_hi * 4 + z_lo), core: 2. Of those that a mesh axis runs over, the one named last changes fastest.
Arguments:
- density: float32 [64, 128, 128], P('gx', 'gy', 'load'), may hold values from 0.05 to 1
- displacement_prior: float32 [16, 3, 64, 128, 128], P('load', None, 'gx', 'gy'), may hold values from -2 to 2
- support: int32 [64, 128, 128], P('gx', 'gy'), may hold values 0 or 1
- load_nodes: int32 [16, 2048], P('load'), may hold values from 0 to 1048575
- load_forces: float32 [16, 3, 2048], P('load'), may hold values from -6 to 6
Outputs:
- displacement: float32 [16, 3, 64, 128, 128], P('load', None, 'gx', 'gy')
- filtered_sensitivity: float32 [64, 128, 128], P('gx', 'gy', 'load')
Inputs may be any that keep to these rules, and one draw needn't show every extreme that they name: `load_nodes`: A node may be named several times; its forces add.
All inputs are finite; a program needn't handle non-finite values. No bound on the sum of `support` on one device may be relied on, other than what follows from the above.
Results may differ from a plain program's by a relative error of at most 0.0001.
Values sent between devices are 32-bit elements; how exact they have to be, the bound alone decides.
A program may use at most 64 MiB of HBM per device.

v0:
```python
import jax
import jax.numpy as jnp
import numpy as np
from jax import lax
from jax.sharding import PartitionSpec as P

SWEEPS = 4
JACOBI = 2


poisson_ratio = 0.3
filter_weight = 3.0
relax_factor = 0.6
modulus_floor = 0.05
block_rows = 4


def extended(cells, sides, width):
    for axis, dim in sides:
        count = lax.axis_size(axis)
        ends = count - 1
        head = lax.slice_in_dim(cells, 0, width, axis=dim)
        tail = lax.slice_in_dim(cells, cells.shape[dim] - width, cells.shape[dim], axis=dim)
        cells = jnp.concatenate(
            [
                lax.ppermute(tail, axis, [(i, (i + 1) % count) for i in range(ends)]),
                cells,
                lax.ppermute(head, axis, [((i + 1) % count, i) for i in range(ends)]),
            ],
            axis=dim,
        )
    return cells


def shifted(value, axis, steps):
    count = lax.axis_size(axis)
    initial, last = (max(0, -steps), min(count, count - steps))
    return lax.ppermute(value, axis, [(source, source + steps) for source in range(initial, last)])


def element_matrix():
    lame_first = poisson_ratio / ((1 + poisson_ratio) * (1 - 2 * poisson_ratio))
    shear = 1.0 / (2 * (1 + poisson_ratio))
    elastic = np.zeros((6, 6))
    elastic[:3, :3] = lame_first
    for index in range(3):
        elastic[index, index] = lame_first + 2 * shear
        elastic[index + 3, index + 3] = shear
    points = [0.5 - 0.5 / np.sqrt(3.0), 0.5 + 0.5 / np.sqrt(3.0)]
    stiffness = np.zeros((24, 24))
    for point_x in points:
        for point_y in points:
            for point_z in points:
                strain = np.zeros((6, 24))
                for corner in range(8):
                    first, second, third = (corner & 1, corner >> 1 & 1, corner >> 2 & 1)
                    shape_x = point_x if first else 1 - point_x
                    shape_y = point_y if second else 1 - point_y
                    shape_z = point_z if third else 1 - point_z
                    slope_x = (1 if first else -1) * shape_y * shape_z
                    slope_y = shape_x * (1 if second else -1) * shape_z
                    slope_z = shape_x * shape_y * (1 if third else -1)
                    column = 3 * corner
                    strain[0, column] = slope_x
                    strain[1, column + 1] = slope_y
                    strain[2, column + 2] = slope_z
                    strain[3, column] = slope_y
                    strain[3, column + 1] = slope_x
                    strain[4, column + 1] = slope_z
                    strain[4, column + 2] = slope_y
                    strain[5, column] = slope_z
                    strain[5, column + 2] = slope_x
                stiffness = stiffness + strain.T @ elastic @ strain / 8.0
    return jnp.asarray(stiffness, dtype=jnp.float32)


def corner_bits(corner):
    return (corner & 1, corner >> 1 & 1, corner >> 2 & 1)


def lane_up(field):
    return jnp.concatenate([field[..., 1:], jnp.zeros_like(field[..., :1])], axis=-1)


def lane_down(field):
    return jnp.concatenate([jnp.zeros_like(field[..., :1]), field[..., :-1]], axis=-1)


def chebyshev(source, extend):
    theta = 1.0 + 6.0 * filter_weight
    delta = 6.0 * filter_weight
    sigma = theta / delta
    result = jnp.zeros_like(source)
    remain = source
    direction = source / theta
    ratio = 1.0 / sigma
    for sweep in range(SWEEPS):
        result = result + direction
        sides, lane_sum = extend(direction)
        beside = sides[2:, 1:-1] + sides[:-2, 1:-1] + sides[1:-1, 2:] + sides[1:-1, :-2] + lane_sum
        remain = remain - ((1.0 + 6.0 * filter_weight) * direction - filter_weight * beside)
        following = 1.0 / (2.0 * sigma - ratio)
        direction = following * ratio * direction + 2.0 * following / delta * remain
        ratio = following
    return result + direction


def brick_extend(field):
    whole = extended(field, (("load", 2), ("gx", 0), ("gy", 1)), 1)
    return (whole[:, :, 1:-1], whole[1:-1, 1:-1, 2:] + whole[1:-1, 1:-1, :-2])


def apply_blocks(ext, modulus_ext, stiff):
    rows = ext.shape[1] - 2
    wide = ext.shape[2] - 2
    raised = lane_up(ext)

    def apply_one_block(index, output):
        start = index * block_rows
        nodes = lax.dynamic_slice_in_dim(ext, start, block_rows + 2, 1)
        nodes_up = lax.dynamic_slice_in_dim(raised, start, block_rows + 2, 1)
        weights = lax.dynamic_slice_in_dim(modulus_ext, start, block_rows + 1, 0)
        pieces = []
        for corner in range(8):
            first, second, third = corner_bits(corner)
            source = nodes_up if third else nodes
            pieces.append(source[:, first : first + block_rows + 1, second : second + wide + 1])
        values = jnp.concatenate(pieces, axis=0)
        forces = (
            jnp.einsum("ij,jxyz->ixyz", stiff, values, precision=lax.Precision.HIGHEST)
            * weights[None]
        )
        summed = jnp.zeros((3, block_rows, wide, ext.shape[3]), jnp.float32)
        for corner in range(8):
            first, second, third = corner_bits(corner)
            piece = forces[
                3 * corner : 3 * corner + 3,
                1 - first : 1 - first + block_rows,
                1 - second : 1 - second + wide,
            ]
            summed = summed + (lane_down(piece) if third else piece)
        return lax.dynamic_update_slice_in_dim(output, summed, start, 1)

    return lax.fori_loop(
        0,
        rows // block_rows,
        apply_one_block,
        jnp.zeros((3, rows, wide, ext.shape[3]), jnp.float32),
    )


def energy_blocks(node_ext, stiff):
    rows = node_ext.shape[1] - 1
    wide = node_ext.shape[2] - 1
    raised = lane_up(node_ext)

    def energy_one_block(index, output):
        start = index * block_rows
        nodes = lax.dynamic_slice_in_dim(node_ext, start, block_rows + 1, 1)
        nodes_up = lax.dynamic_slice_in_dim(raised, start, block_rows + 1, 1)
        pieces = []
        for corner in range(8):
            first, second, third = corner_bits(corner)
            source = nodes_up if third else nodes
            pieces.append(source[:, first : first + block_rows, second : second + wide])
        values = jnp.concatenate(pieces, axis=0)
        product = jnp.einsum("ij,jxyz->ixyz", stiff, values, precision=lax.Precision.HIGHEST)
        return lax.dynamic_update_slice_in_dim(output, jnp.sum(values * product, axis=0), start, 0)

    return lax.fori_loop(
        0,
        rows // block_rows,
        energy_one_block,
        jnp.zeros((rows, wide, node_ext.shape[3]), jnp.float32),
    )


def body(density, displacement_prior, support, load_nodes, load_forces):
    stiff = element_matrix()
    rows, wide, depth = support.shape
    cases = lax.axis_size("load")
    filtered = lax.all_gather(chebyshev(density, brick_extend), "load", axis=2, tiled=True)
    modulus = modulus_floor + filtered * filtered
    lower_row = shifted(modulus[-1:], "gx", 1)
    widened = jnp.concatenate([lower_row, modulus], axis=0)
    lower_column = shifted(widened[:, -1:], "gy", 1)
    modulus_ext = jnp.concatenate([lower_column, widened], axis=1)
    modulus_low = lane_down(modulus_ext)
    free = (1 - support).astype(jnp.float32)
    diag_entries = jnp.diagonal(stiff)
    parts = []
    for component in range(3):
        total = jnp.zeros((rows, wide, depth), jnp.float32)
        for corner in range(8):
            first, second, third = corner_bits(corner)
            source = modulus_low if third else modulus_ext
            total = (
                total
                + source[1 - first : 1 - first + rows, 1 - second : 1 - second + wide]
                * diag_entries[3 * corner + component]
            )
        parts.append(total)
    diagonal = jnp.stack(parts)
    total_c = wide * lax.axis_size("gy")
    nodes = load_nodes[0]
    node_row = nodes // (total_c * depth) - lax.axis_index("gx") * rows
    node_column = nodes // depth % total_c - lax.axis_index("gy") * wide
    node_depth = nodes % depth
    inside = (node_row >= 0) & (node_row < rows) & (node_column >= 0) & (node_column < wide)
    local_index = jnp.where(
        inside, (node_row * wide + node_column) * depth + node_depth, rows * wide * depth
    )
    flat_force = (
        jnp.zeros((3, rows * wide * depth), jnp.float32)
        .at[:, local_index]
        .add(load_forces[0], mode="drop")
    )
    force = flat_force.reshape((3, rows, wide, depth))
    field = displacement_prior[0]
    for sweep in range(JACOBI):
        ext = extended(field, (("gx", 1), ("gy", 2)), 1)
        applied = apply_blocks(ext, modulus_ext, stiff)
        field = free * (field + relax_factor * (force - applied) / diagonal)
    upper_x = shifted(field[:, :1], "gx", -1)
    section = jnp.concatenate([field, upper_x], axis=1)
    upper_y = shifted(section[:, :, :1], "gy", -1)
    node_ext = jnp.concatenate([section, upper_y], axis=2)
    energy = energy_blocks(node_ext, stiff)
    term = -(2.0 / cases) * filtered * energy
    share = lax.psum_scatter(term, "load", scatter_dimension=2, tiled=True)
    result = chebyshev(share, brick_extend)
    return (field[None], result)


def solution(mesh):
    return jax.shard_map(
        body,
        mesh=mesh,
        in_specs=(
            P("gx", "gy", "load"),
            P("load", None, "gx", "gy", None),
            P("gx", "gy", None),
            P("load", None),
            P("load", None, None),
        ),
        out_specs=(P("load", None, "gx", "gy", None), P("gx", "gy", "load")),
        check_vma=False,
    )
```

profile of v0, /device:TPU:1, one launch (start us, length us, event | category | flops | bytes accessed | tf_op | source)
XLA Modules:
  0.0 663.1 jit_solution(1652304117906738498)
XLA Ops:
  8.1 4.0 collective-permute-start.4
  13.4 3.0 collective-permute-done.5
  16.4 7.2 %collective-permute-start.6 = (f32[1,32,10]{1,0,2:T(1,128)S(1)}, f32[1,32,10]{1,0,2:T(1,128)S(1)}, u32[]{:S(2)}, u32[]{:S(2)}) collective-permute-start(f32[1,32,10]{1,0,2:T(1,128)S(1)} %get-tuple-element.569), channel_id=1, source_target_pairs={{4,0},{8,4},{12,8},{16,12},{20,16},{24,20},{28,24},{5,1},{9,5},{13... | collective-permute-start | bytes 3848 | tf_op jit(solution)/shard_map/ppermute | solution.py:28
  26.8 6.8 %collective-permute-start.9 = (f32[10,1,10]{1,0,2:T(8,128)S(1)}, f32[10,1,10]{1,0,2:T(8,128)S(1)}, u32[]{:S(2)}, u32[]{:S(2)}) collective-permute-start(f32[10,1,10]{1,0,2:T(8,128)S(1)} %get-tuple-element.553), channel_id=1, source_target_pairs={{0,1},{1,2},{2,3},{4,5},{5,6},{6,7},{8,9},{9,10},{10,11},{12,13},{... | collective-permute-start | bytes 1208 | tf_op jit(solution)/shard_map/ppermute | solution.py:26
  35.4 12.8 %collective-permute-done.8 = f32[10,1,10]{1,0,2:T(8,128)S(1)} collective-permute-done((f32[10,1,10]{1,0,2:T(8,128)S(1)}, f32[10,1,10]{1,0,2:T(8,128)S(1)}, u32[]{:S(2)}, u32[]{:S(2)}) %collective-permute-start.8) | collective-permute-done | bytes 432 | tf_op jit(solution)/shard_map/ppermute | solution.py:28
  49.0 3.2 collective-permute-start.10
  53.5 3.0 collective-permute-done.11
  56.6 4.8 collective-permute-start.12
  64.6 7.9 %collective-permute-start.15 = (f32[10,1,10]{1,0,2:T(8,128)S(1)}, f32[10,1,10]{1,0,2:T(8,128)S(1)}, u32[]{:S(2)}, u32[]{:S(2)}) collective-permute-start(f32[10,1,10]{1,0,2:T(8,128)S(1)} %get-tuple-element.551), channel_id=1, source_target_pairs={{0,1},{1,2},{2,3},{4,5},{5,6},{6,7},{8,9},{9,10},{10,11},{12,13},{... | collective-permute-start | bytes 1208 | tf_op jit(solution)/shard_map/ppermute | solution.py:26
  74.1 12.5 %collective-permute-done.14 = f32[10,1,10]{1,0,2:T(8,128)S(1)} collective-permute-done((f32[10,1,10]{1,0,2:T(8,128)S(1)}, f32[10,1,10]{1,0,2:T(8,128)S(1)}, u32[]{:S(2)}, u32[]{:S(2)}) %collective-permute-start.14) | collective-permute-done | bytes 432 | tf_op jit(solution)/shard_map/ppermute | solution.py:28
  86.7 4.3 collective-permute-start.16
  92.4 3.2 collective-permute-done.17
  95.5 3.7 collective-permute-start.18
  104.4 3.2 collective-permute-start
  107.7 2.9 collective-permute-start.21
  112.6 11.9 %collective-permute-done.20 = f32[10,1,10]{1,0,2:T(8,128)S(1)} collective-permute-done((f32[10,1,10]{1,0,2:T(8,128)S(1)}, f32[10,1,10]{1,0,2:T(8,128)S(1)}, u32[]{:S(2)}, u32[]{:S(2)}) %collective-permute-start.20) | collective-permute-done | bytes 432 | tf_op jit(solution)/shard_map/ppermute | solution.py:28
  124.6 3.8 collective-permute-start.22
  129.8 3.2 collective-permute-done.23
  133.0 3.5 collective-permute-start.24
  139.6 3.5 collective-permute-start.27
  145.3 11.2 %collective-permute-done.26 = f32[10,1,10]{1,0,2:T(8,128)S(1)} collective-permute-done((f32[10,1,10]{1,0,2:T(8,128)S(1)}, f32[10,1,10]{1,0,2:T(8,128)S(1)}, u32[]{:S(2)}, u32[]{:S(2)}) %collective-permute-start.26) | collective-permute-done | bytes 432 | tf_op jit(solution)/shard_map/ppermute | solution.py:28
  156.6 20.9 %all_gather.3 = f32[8,32,128]{1,0,2:T(8,128)S(1)} all-gather(f32[8,32,8]{1,0,2:T(8,128)S(1)} %fusion.51), channel_id=1, replica_groups=mesh['load'=16,'gx'=8,'gy'=4] {'load'}, dimensions={2}, use_global_device_ids=true | all-gather | bytes 139264 | tf_op jit(solution)/shard_map/all_gather | solution.py:182
  177.7 9.8 %collective-permute-start.28 = (f32[1,32,128]{2,1,0:T(8,128)S(1)}, f32[1,32,128]{2,1,0:T(8,128)S(1)}, u32[]{:S(2)}, u32[]{:S(2)}) collective-permute-start(f32[1,32,128]{2,1,0:T(8,128)S(1)} %slice.1119), channel_id=1, source_target_pairs={{0,4},{4,8},{8,12},{12,16},{16,20},{20,24},{24,28},{1,5},{5,9},{9,... | collective-permute-start | bytes 49160 | tf_op jit(solution)/shard_map/ppermute | solution.py:38
  190.7 18.3 %scatter_custom_fusion = f32[3,32768]{0,1:T(8,128)} fusion(s32[2048]{0:T(1024)S(1)} %bitcast.105, f32[2048,3]{1,0:T(8,128)S(1)} %copy.126, f32[]{:T(128)} %constant.217.clone.1), kind=kCustom, calls=%fused_computation.49 | custom fusion | flops 6144 | bytes 393220 | tf_op jit(solution)/shard_map/scatter-add | solution.py:216
  209.0 10.6 %copy.135 = f32[3,8,32,128]{3,2,1,0:T(8,128)} copy(f32[3,8,32,128]{0,3,2,1:T(8,128)} %bitcast.96) | data formatting | bytes 786432 | tf_op jit(solution)/shard_map/reshape | solution.py:218
  219.7 6.0 add_bitcast_fusion
  225.7 5.9 add_bitcast_fusion.1
  232.9 8.1 %collective-permute-start.2 = (f32[3,10,1,128]{3,2,1,0:T(1,128)S(1)}, f32[3,10,1,128]{3,2,1,0:T(1,128)S(1)}, u32[]{:S(2)}, u32[]{:S(2)}) collective-permute-start(f32[3,10,1,128]{3,2,1,0:T(1,128)S(1)} %get-tuple-element.532), channel_id=1, source_target_pairs={{0,1},{1,2},{2,3},{4,5},{5,6},{6,7},{8,9},{9,10},{10,11},{12,13},{... | collective-permute-start | bytes 46088 | tf_op jit(solution)/shard_map/ppermute | solution.py:26
  241.0 5.8 add_bitcast_fusion.2
  248.0 57.1 %while.42 = (s32[]{:T(128)}, f32[3,8,32,128]{3,2,1,0:T(8,128)}, f32[3,10,34,128]{3,2,1,0:T(8,128)S(1)}, f32[3,10,34,128]{3,2,1,0:T(8,128)S(1)}, f32[9,33,128]{2,...) while((s32[]{:T(128)}, f32[3,8,32,128]{3,2,1,0:T(8,128)}, ...), condition=%wide.region_2.3_spmd.clone, body=%wide.region_1.2_spmd.sunk.clone.sunk | while | flops 146832400 | bytes 23404616 | solution.py:144
  254.7 18.1 %concatenate.453 = f32[24,5,33,128]{3,0,2,1:T(8,128)S(1)} concatenate(f32[3,5,33,128]{3,0,2,1:T(4,128)} %copy.225, f32[3,5,33,128]{3,0,2,1:T(4,128)} %copy.226, f32[3,5,33,128]{3,0,2,1:T(4,128)} %copy.227, f32[3,5,33,128]{3,0,2,1:T(4,128)} %copy.228, f32[3,5,33,128]{3,0,2,1:T(4,128)} %copy.229, f32[3,5,33,128]{3,0,2,1:T(4,128)} %copy.230, f32[3,5,33,128]{3,0,2,1:T(4,128)} %copy.231, ...), dimensions={0} | concatenate | bytes 4055040 | tf_op jit(solution)/shard_map/while/body/eval_jaxpr/concatenate | solution.py:128
  283.2 18.1 %concatenate.453 = f32[24,5,33,128]{3,0,2,1:T(8,128)S(1)} concatenate(f32[3,5,33,128]{3,0,2,1:T(4,128)} %copy.225, f32[3,5,33,128]{3,0,2,1:T(4,128)} %copy.226, f32[3,5,33,128]{3,0,2,1:T(4,128)} %copy.227, f32[3,5,33,128]{3,0,2,1:T(4,128)} %copy.228, f32[3,5,33,128]{3,0,2,1:T(4,128)} %copy.229, f32[3,5,33,128]{3,0,2,1:T(4,128)} %copy.230, f32[3,5,33,128]{3,0,2,1:T(4,128)} %copy.231, ...), dimensions={0} | concatenate | bytes 4055040 | tf_op jit(solution)/shard_map/while/body/eval_jaxpr/concatenate | solution.py:128
  308.5 4.8 collective-permute-start.30
  315.8 7.9 %collective-permute-start.32 = (f32[3,10,1,128]{3,2,1,0:T(1,128)S(1)}, f32[3,10,1,128]{3,2,1,0:T(1,128)S(1)}, u32[]{:S(2)}, u32[]{:S(2)}) collective-permute-start(f32[3,10,1,128]{3,2,1,0:T(1,128)S(1)} %get-tuple-element.530), channel_id=1, source_target_pairs={{0,1},{1,2},{2,3},{4,5},{5,6},{6,7},{8,9},{9,10},{10,11},{12,13},{... | collective-permute-start | bytes 46088 | tf_op jit(solution)/shard_map/ppermute | solution.py:26
  325.7 57.1 %while.43 = (s32[]{:T(128)}, f32[3,8,32,128]{3,2,1,0:T(8,128)}, f32[3,10,34,128]{3,2,1,0:T(8,128)S(1)}, f32[3,10,34,128]{3,2,1,0:T(8,128)S(1)}, f32[9,33,128]{2,...) while((s32[]{:T(128)}, f32[3,8,32,128]{3,2,1,0:T(8,128)}, ...), condition=%wide.region_4.5_spmd.clone, body=%wide.region_3.4_spmd.sunk.clone.sunk | while | flops 146832400 | bytes 23404616 | solution.py:144
  332.5 18.1 %concatenate.458 = f32[24,5,33,128]{3,0,2,1:T(8,128)S(1)} concatenate(f32[3,5,33,128]{3,0,2,1:T(4,128)} %copy.234, f32[3,5,33,128]{3,0,2,1:T(4,128)} %copy.235, f32[3,5,33,128]{3,0,2,1:T(4,128)} %copy.236, f32[3,5,33,128]{3,0,2,1:T(4,128)} %copy.237, f32[3,5,33,128]{3,0,2,1:T(4,128)} %copy.238, f32[3,5,33,128]{3,0,2,1:T(4,128)} %copy.239, f32[3,5,33,128]{3,0,2,1:T(4,128)} %copy.240, ...), dimensions={0} | concatenate | bytes 4055040 | tf_op jit(solution)/shard_map/while/body/eval_jaxpr/concatenate | solution.py:128
  361.1 18.1 %concatenate.458 = f32[24,5,33,128]{3,0,2,1:T(8,128)S(1)} concatenate(f32[3,5,33,128]{3,0,2,1:T(4,128)} %copy.234, f32[3,5,33,128]{3,0,2,1:T(4,128)} %copy.235, f32[3,5,33,128]{3,0,2,1:T(4,128)} %copy.236, f32[3,5,33,128]{3,0,2,1:T(4,128)} %copy.237, f32[3,5,33,128]{3,0,2,1:T(4,128)} %copy.238, f32[3,5,33,128]{3,0,2,1:T(4,128)} %copy.239, f32[3,5,33,128]{3,0,2,1:T(4,128)} %copy.240, ...), dimensions={0} | concatenate | bytes 4055040 | tf_op jit(solution)/shard_map/while/body/eval_jaxpr/concatenate | solution.py:128
  386.4 5.2 collective-permute-done.34
  393.1 7.5 %collective-permute-done.35 = f32[3,9,1,128]{3,2,1,0:T(1,128)S(1)} collective-permute-done((f32[3,9,1,128]{3,2,1,0:T(1,128)S(1)}, f32[3,9,1,128]{3,2,1,0:T(1,128)S(1)}, u32[]{:S(2)}, u32[]{:S(2)}) %collective-permute-start.35) | collective-permute-done | bytes 13856 | tf_op jit(solution)/shard_map/ppermute | solution.py:38
  401.6 29.3 %while.44 = (s32[]{:T(128)}, f32[8,32,128]{2,1,0:T(8,128)}, f32[3,9,33,128]{3,2,1,0:T(8,128)S(1)}, f32[3,9,33,128]{3,2,1,0:T(8,128)S(1)}, s32[]{:T(128)}, /*inde...) while((s32[]{:T(128)}, f32[8,32,128]{2,1,0:T(8,128)}, ...), condition=%wide.region_7.8_spmd.clone, body=%wide.region_5.7_spmd.sunk.clone.sunk | while | flops 114016264 | bytes 11209188 | solution.py:170
  406.6 7.5 %concatenate.459 = f32[24,4,32,128]{3,0,2,1:T(8,128)S(1)} concatenate(f32[3,4,32,128]{3,0,2,1:T(4,128)S(1)} %copy.242, f32[3,4,32,128]{3,0,2,1:T(4,128)S(1)} %copy.243, f32[3,4,32,128]{3,0,2,1:T(4,128)S(1)} %copy.244, f32[3,4,32,128]{3,0,2,1:T(4,128)} %copy.245, f32[3,4,32,128]{3,0,2,1:T(4,128)} %copy.246, f32[3,4,32,128]{3,0,2,1:T(4,128)} %copy.247, f32[3,4,32,128]{3,0,2,1:T(4,128)} %copy.248, ...), dimensions={0} | concatenate | bytes 3145728 | tf_op jit(solution)/shard_map/while/body/eval_jaxpr/concatenate | solution.py:166
  421.2 7.5 %concatenate.459 = f32[24,4,32,128]{3,0,2,1:T(8,128)S(1)} concatenate(f32[3,4,32,128]{3,0,2,1:T(4,128)S(1)} %copy.242, f32[3,4,32,128]{3,0,2,1:T(4,128)S(1)} %copy.243, f32[3,4,32,128]{3,0,2,1:T(4,128)S(1)} %copy.244, f32[3,4,32,128]{3,0,2,1:T(4,128)} %copy.245, f32[3,4,32,128]{3,0,2,1:T(4,128)} %copy.246, f32[3,4,32,128]{3,0,2,1:T(4,128)} %copy.247, f32[3,4,32,128]{3,0,2,1:T(4,128)} %copy.248, ...), dimensions={0} | concatenate | bytes 3145728 | tf_op jit(solution)/shard_map/while/body/eval_jaxpr/concatenate | solution.py:166
  432.9 83.4 %reduce-scatter.2.cloned.1.call-done = f32[8,32,8]{1,0,2:T(8,128)} async-done(((f32[8,32,128]{1,0,2:T(8,128)}), f32[8,32,8]{1,0,2:T(8,128)}) %reduce-scatter.2.cloned.1.call-update) | async-done | bytes 8208 | tf_op jit(solution)/shard_map/reduce_scatter | solution.py:230
  517.2 2.4 collective-permute-start.36
  520.9 3.0 collective-permute-done.37
  524.0 6.0 collective-permute-start.38
  530.0 3.1 collective-permute-start.39
  534.0 7.4 %collective-permute-start.41 = (f32[10,1,10]{1,0,2:T(8,128)S(1)}, f32[10,1,10]{1,0,2:T(8,128)S(1)}, u32[]{:S(2)}, u32[]{:S(2)}) collective-permute-start(f32[10,1,10]{1,0,2:T(8,128)S(1)} %get-tuple-element.545), channel_id=1, source_target_pairs={{0,1},{1,2},{2,3},{4,5},{5,6},{6,7},{8,9},{9,10},{10,11},{12,13},{... | collective-permute-start | bytes 1208 | tf_op jit(solution)/shard_map/ppermute | solution.py:26
  543.5 13.2 %collective-permute-done.40 = f32[10,1,10]{1,0,2:T(8,128)S(1)} collective-permute-done((f32[10,1,10]{1,0,2:T(8,128)S(1)}, f32[10,1,10]{1,0,2:T(8,128)S(1)}, u32[]{:S(2)}, u32[]{:S(2)}) %collective-permute-start.40) | collective-permute-done | bytes 432 | tf_op jit(solution)/shard_map/ppermute | solution.py:28
  557.6 3.0 collective-permute-start.42
  562.0 3.0 collective-permute-done.43
  565.0 3.9 collective-permute-start.44
  572.1 6.6 collective-permute-start.47
  580.3 10.5 %collective-permute-done.46 = f32[10,1,10]{1,0,2:T(8,128)S(1)} collective-permute-done((f32[10,1,10]{1,0,2:T(8,128)S(1)}, f32[10,1,10]{1,0,2:T(8,128)S(1)}, u32[]{:S(2)}, u32[]{:S(2)}) %collective-permute-start.46) | collective-permute-done | bytes 432 | tf_op jit(solution)/shard_map/ppermute | solution.py:28
  594.3 3.3 collective-permute-done.49
  597.6 6.3 collective-permute-start.50
  603.9 3.2 collective-permute-start.51
  608.0 2.8 collective-permute-start.53
  612.8 11.0 %collective-permute-done.52 = f32[10,1,10]{1,0,2:T(8,128)S(1)} collective-permute-done((f32[10,1,10]{1,0,2:T(8,128)S(1)}, f32[10,1,10]{1,0,2:T(8,128)S(1)}, u32[]{:S(2)}, u32[]{:S(2)}) %collective-permute-start.52) | collective-permute-done | bytes 432 | tf_op jit(solution)/shard_map/ppermute | solution.py:28
  624.0 3.7 collective-permute-start.54
  629.0 3.5 collective-permute-done.55
  632.5 3.5 collective-permute-start.56
  636.0 3.8 collective-permute-start.57
  644.0 11.6 %collective-permute-done.58 = f32[10,1,10]{1,0,2:T(8,128)S(1)} collective-permute-done((f32[10,1,10]{1,0,2:T(8,128)S(1)}, f32[10,1,10]{1,0,2:T(8,128)S(1)}, u32[]{:S(2)}, u32[]{:S(2)}) %collective-permute-start.58) | collective-permute-done | bytes 432 | tf_op jit(solution)/shard_map/ppermute | solution.py:28
  (268 shorter events, 131.9 us)
Async XLA Ops:
  7.2 137.3 %copy-start = (f32[24,24]{1,0:T(8,128)S(1)}, f32[24,24]{1,0:T(8,128)}, u32[]{:S(2)}) copy-start(f32[24,24]{1,0:T(8,128)} %constant.245.clone) | copy-start | bytes 6916
  7.2 509.1 %reduce-scatter.2.cloned.1.call-start = ((), (), s32[]{:S(2)}) async-start(), calls=%async_computation.1 | async-start | bytes 557056 | tf_op jit(solution)/shard_map/reduce_scatter | solution.py:230
  8.1 5.3 collective-permute-start.4
  12.1 4.4 collective-permute-start.5
  16.4 9.1 %collective-permute-start.6 = (f32[1,32,10]{1,0,2:T(1,128)S(1)}, f32[1,32,10]{1,0,2:T(1,128)S(1)}, u32[]{:S(2)}, u32[]{:S(2)}) collective-permute-start(f32[1,32,10]{1,0,2:T(1,128)S(1)} %get-tuple-element.569), channel_id=1, source_target_pairs={{4,0},{8,4},{12,8},{16,12},{20,16},{24,20},{28,24},{5,1},{9,5},{13... | collective-permute-start | bytes 3848 | tf_op jit(solution)/shard_map/ppermute | solution.py:28
  23.6 132.8 %copy-start.10 = (f32[8,32,8]{1,2,0:T(8,128)S(1)}, f32[8,32,8]{1,2,0:T(8,128)}, u32[]{:S(2)}) copy-start(f32[8,32,8]{1,2,0:T(8,128)} %param.12) | copy-start | bytes 24580
  23.6 3.1 collective-permute-start.7
  26.8 8.5 %collective-permute-start.9 = (f32[10,1,10]{1,0,2:T(8,128)S(1)}, f32[10,1,10]{1,0,2:T(8,128)S(1)}, u32[]{:S(2)}, u32[]{:S(2)}) collective-permute-start(f32[10,1,10]{1,0,2:T(8,128)S(1)} %get-tuple-element.553), channel_id=1, source_target_pairs={{0,1},{1,2},{2,3},{4,5},{5,6},{6,7},{8,9},{9,10},{10,11},{12,13},{... | collective-permute-start | bytes 1208 | tf_op jit(solution)/shard_map/ppermute | solution.py:26
  33.6 14.5 %collective-permute-start.8 = (f32[10,1,10]{1,0,2:T(8,128)S(1)}, f32[10,1,10]{1,0,2:T(8,128)S(1)}, u32[]{:S(2)}, u32[]{:S(2)}) collective-permute-start(f32[10,1,10]{1,0,2:T(8,128)S(1)} %get-tuple-element.552), channel_id=1, source_target_pairs={{1,0},{2,1},{3,2},{5,4},{6,5},{7,6},{9,8},{10,9},{11,10},{13,12},{... | collective-permute-start | bytes 1208 | tf_op jit(solution)/shard_map/ppermute | solution.py:28
  49.0 4.5 collective-permute-start.10
  52.2 4.4 collective-permute-start.11
  56.6 6.9 %collective-permute-start.12 = (f32[1,32,10]{1,0,2:T(1,128)S(1)}, f32[1,32,10]{1,0,2:T(1,128)S(1)}, u32[]{:S(2)}, u32[]{:S(2)}) collective-permute-start(f32[1,32,10]{1,0,2:T(1,128)S(1)} %get-tuple-element.567), channel_id=1, source_target_pairs={{4,0},{8,4},{12,8},{16,12},{20,16},{24,20},{28,24},{5,1},{9,5},{13... | collective-permute-start | bytes 3848 | tf_op jit(solution)/shard_map/ppermute | solution.py:28
  61.4 3.1 collective-permute-start.13
  64.6 9.5 %collective-permute-start.15 = (f32[10,1,10]{1,0,2:T(8,128)S(1)}, f32[10,1,10]{1,0,2:T(8,128)S(1)}, u32[]{:S(2)}, u32[]{:S(2)}) collective-permute-start(f32[10,1,10]{1,0,2:T(8,128)S(1)} %get-tuple-element.551), channel_id=1, source_target_pairs={{0,1},{1,2},{2,3},{4,5},{5,6},{6,7},{8,9},{9,10},{10,11},{12,13},{... | collective-permute-start | bytes 1208 | tf_op jit(solution)/shard_map/ppermute | solution.py:26
  72.5 14.1 %collective-permute-start.14 = (f32[10,1,10]{1,0,2:T(8,128)S(1)}, f32[10,1,10]{1,0,2:T(8,128)S(1)}, u32[]{:S(2)}, u32[]{:S(2)}) collective-permute-start(f32[10,1,10]{1,0,2:T(8,128)S(1)} %get-tuple-element.550), channel_id=1, source_target_pairs={{1,0},{2,1},{3,2},{5,4},{6,5},{7,6},{9,8},{10,9},{11,10},{13,12},{... | collective-permute-start | bytes 1208 | tf_op jit(solution)/shard_map/ppermute | solution.py:28
  86.7 5.6 collective-permute-start.16
  91.0 4.5 collective-permute-start.17
  95.5 12.1 %collective-permute-start.18 = (f32[1,32,10]{1,0,2:T(1,128)S(1)}, f32[1,32,10]{1,0,2:T(1,128)S(1)}, u32[]{:S(2)}, u32[]{:S(2)}) collective-permute-start(f32[1,32,10]{1,0,2:T(1,128)S(1)} %get-tuple-element.565), channel_id=1, source_target_pairs={{4,0},{8,4},{12,8},{16,12},{20,16},{24,20},{28,24},{5,1},{9,5},{13... | collective-permute-start | bytes 3848 | tf_op jit(solution)/shard_map/ppermute | solution.py:28
  99.2 8.4 %collective-permute-start.19 = (f32[1,32,10]{1,0,2:T(1,128)S(1)}, f32[1,32,10]{1,0,2:T(1,128)S(1)}, u32[]{:S(2)}, u32[]{:S(2)}) collective-permute-start(f32[1,32,10]{1,0,2:T(1,128)S(1)} %get-tuple-element.564), channel_id=1, source_target_pairs={{0,4},{4,8},{8,12},{12,16},{16,20},{20,24},{24,28},{1,5},{5,9},{9,... | collective-permute-start | bytes 3848 | tf_op jit(solution)/shard_map/ppermute | solution.py:26
  102.0 129.5 %collective-permute-start.1 = (f32[3,1,32,128]{3,2,1,0:T(8,128)S(1)}, f32[3,1,32,128]{3,2,1,0:T(8,128)S(1)}, u32[]{:S(2)}, u32[]{:S(2)}) collective-permute-start(f32[3,1,32,128]{3,2,1,0:T(8,128)S(1)} %get-tuple-element.537), channel_id=1, source_target_pairs={{4,0},{8,4},{12,8},{16,12},{20,16},{24,20},{28,24},{5,1},{9,5},{13... | collective-permute-start | bytes 147464 | tf_op jit(solution)/shard_map/ppermute | solution.py:28
  104.4 127.1 %collective-permute-start = (f32[3,1,32,128]{3,2,1,0:T(8,128)S(1)}, f32[3,1,32,128]{3,2,1,0:T(8,128)S(1)}, u32[]{:S(2)}, u32[]{:S(2)}) collective-permute-start(f32[3,1,32,128]{3,2,1,0:T(8,128)S(1)} %get-tuple-element.536), channel_id=1, source_target_pairs={{0,4},{4,8},{8,12},{12,16},{16,20},{20,24},{24,28},{1,5},{5,9},{9,... | collective-permute-start | bytes 147464 | tf_op jit(solution)/shard_map/ppermute | solution.py:26
  107.7 4.8 collective-permute-start.21
  110.6 13.9 %collective-permute-start.20 = (f32[10,1,10]{1,0,2:T(8,128)S(1)}, f32[10,1,10]{1,0,2:T(8,128)S(1)}, u32[]{:S(2)}, u32[]{:S(2)}) collective-permute-start(f32[10,1,10]{1,0,2:T(8,128)S(1)} %get-tuple-element.548), channel_id=1, source_target_pairs={{1,0},{2,1},{3,2},{5,4},{6,5},{7,6},{9,8},{10,9},{11,10},{13,12},{... | collective-permute-start | bytes 1208 | tf_op jit(solution)/shard_map/ppermute | solution.py:28
  124.6 5.2 collective-permute-start.22
  128.4 4.6 collective-permute-start.23
  133.0 6.2 collective-permute-start.24
  136.5 3.1 collective-permute-start.25
  139.6 5.6 collective-permute-start.27
  143.1 13.3 %collective-permute-start.26 = (f32[10,1,10]{1,0,2:T(8,128)S(1)}, f32[10,1,10]{1,0,2:T(8,128)S(1)}, u32[]{:S(2)}, u32[]{:S(2)}) collective-permute-start(f32[10,1,10]{1,0,2:T(8,128)S(1)} %get-tuple-element.546), channel_id=1, source_target_pairs={{1,0},{2,1},{3,2},{5,4},{6,5},{7,6},{9,8},{10,9},{11,10},{13,12},{... | collective-permute-start | bytes 1208 | tf_op jit(solution)/shard_map/ppermute | solution.py:28
  177.7 10.6 %collective-permute-start.28 = (f32[1,32,128]{2,1,0:T(8,128)S(1)}, f32[1,32,128]{2,1,0:T(8,128)S(1)}, u32[]{:S(2)}, u32[]{:S(2)}) collective-permute-start(f32[1,32,128]{2,1,0:T(8,128)S(1)} %slice.1119), channel_id=1, source_target_pairs={{0,4},{4,8},{8,12},{12,16},{16,20},{20,24},{24,28},{1,5},{5,9},{9,... | collective-permute-start | bytes 49160 | tf_op jit(solution)/shard_map/ppermute | solution.py:38
  188.3 31.3 %collective-permute-start.29 = (f32[9,1,128]{2,1,0:T(1,128)S(1)}, f32[9,1,128]{2,1,0:T(1,128)S(1)}, u32[]{:S(2)}, u32[]{:S(2)}) collective-permute-start(f32[9,1,128]{2,1,0:T(1,128)S(1)} %pad_maximum_fusion.188), channel_id=1, source_target_pairs={{0,1},{1,2},{2,3},{4,5},{5,6},{6,7},{8,9},{9,10},{10,11},{12,13},{... | collective-permute-start | bytes 13832 | tf_op jit(solution)/shard_map/ppermute | solution.py:38
  231.6 15.2 %collective-permute-start.3 = (f32[3,10,1,128]{3,2,1,0:T(1,128)S(1)}, f32[3,10,1,128]{3,2,1,0:T(1,128)S(1)}, u32[]{:S(2)}, u32[]{:S(2)}) collective-permute-start(f32[3,10,1,128]{3,2,1,0:T(1,128)S(1)} %get-tuple-element.533), channel_id=1, source_target_pairs={{1,0},{2,1},{3,2},{5,4},{6,5},{7,6},{9,8},{10,9},{11,10},{13,12},{... | collective-permute-start | bytes 46088 | tf_op jit(solution)/shard_map/ppermute | solution.py:28
  232.9 13.9 %collective-permute-start.2 = (f32[3,10,1,128]{3,2,1,0:T(1,128)S(1)}, f32[3,10,1,128]{3,2,1,0:T(1,128)S(1)}, u32[]{:S(2)}, u32[]{:S(2)}) collective-permute-start(f32[3,10,1,128]{3,2,1,0:T(1,128)S(1)} %get-tuple-element.532), channel_id=1, source_target_pairs={{0,1},{1,2},{2,3},{4,5},{5,6},{6,7},{8,9},{9,10},{10,11},{12,13},{... | collective-permute-start | bytes 46088 | tf_op jit(solution)/shard_map/ppermute | solution.py:26
  306.6 6.7 %collective-permute-start.31 = (f32[3,1,32,128]{3,2,1,0:T(8,128)S(1)}, f32[3,1,32,128]{3,2,1,0:T(8,128)S(1)}, u32[]{:S(2)}, u32[]{:S(2)}) collective-permute-start(f32[3,1,32,128]{3,2,1,0:T(8,128)S(1)} %get-tuple-element.535), channel_id=1, source_target_pairs={{4,0},{8,4},{12,8},{16,12},{20,16},{24,20},{28,24},{5,1},{9,5},{13... | collective-permute-start | bytes 147464 | tf_op jit(solution)/shard_map/ppermute | solution.py:28
  308.5 5.9 collective-permute-start.30
  314.5 9.2 %collective-permute-start.33 = (f32[3,10,1,128]{3,2,1,0:T(1,128)S(1)}, f32[3,10,1,128]{3,2,1,0:T(1,128)S(1)}, u32[]{:S(2)}, u32[]{:S(2)}) collective-permute-start(f32[3,10,1,128]{3,2,1,0:T(1,128)S(1)} %get-tuple-element.531), channel_id=1, source_target_pairs={{1,0},{2,1},{3,2},{5,4},{6,5},{7,6},{9,8},{10,9},{11,10},{13,12},{... | collective-permute-start | bytes 46088 | tf_op jit(solution)/shard_map/ppermute | solution.py:28
  315.8 8.7 %collective-permute-start.32 = (f32[3,10,1,128]{3,2,1,0:T(1,128)S(1)}, f32[3,10,1,128]{3,2,1,0:T(1,128)S(1)}, u32[]{:S(2)}, u32[]{:S(2)}) collective-permute-start(f32[3,10,1,128]{3,2,1,0:T(1,128)S(1)} %get-tuple-element.530), channel_id=1, source_target_pairs={{0,1},{1,2},{2,3},{4,5},{5,6},{6,7},{8,9},{9,10},{10,11},{12,13},{... | collective-permute-start | bytes 46088 | tf_op jit(solution)/shard_map/ppermute | solution.py:26
  384.4 7.1 %collective-permute-start.34 = (f32[3,1,32,128]{3,2,1,0:T(8,128)S(1)}, f32[3,1,32,128]{3,2,1,0:T(8,128)S(1)}, u32[]{:S(2)}, u32[]{:S(2)}) collective-permute-start(f32[3,1,32,128]{3,2,1,0:T(8,128)S(1)} %slice.1126), channel_id=1, source_target_pairs={{4,0},{8,4},{12,8},{16,12},{20,16},{24,20},{28,24},{5,1},{9,5},{13... | collective-permute-start | bytes 147464 | tf_op jit(solution)/shard_map/ppermute | solution.py:38
  391.6 9.1 %collective-permute-start.35 = (f32[3,9,1,128]{3,2,1,0:T(1,128)S(1)}, f32[3,9,1,128]{3,2,1,0:T(1,128)S(1)}, u32[]{:S(2)}, u32[]{:S(2)}) collective-permute-start(f32[3,9,1,128]{3,2,1,0:T(1,128)S(1)} %pad_maximum_fusion.163), channel_id=1, source_target_pairs={{1,0},{2,1},{3,2},{5,4},{6,5},{7,6},{9,8},{10,9},{11,10},{13,12},{... | collective-permute-start | bytes 41480 | tf_op jit(solution)/shard_map/ppermute | solution.py:38
  516.3 139.2 %copy-start.11 = (f32[8,32,8]{1,0,2:T(8,128)S(1)}, f32[8,32,8]{1,0,2:T(8,128)}, u32[]{:S(2)}) copy-start(f32[8,32,8]{1,0,2:T(8,128)} %reduce-scatter.2.cloned.1.call-done) | copy-start | bytes 24580
  517.2 3.7 collective-permute-start.36
  519.6 4.4 collective-permute-start.37
  524.0 9.1 %collective-permute-start.38 = (f32[1,32,10]{1,0,2:T(1,128)S(1)}, f32[1,32,10]{1,0,2:T(1,128)S(1)}, u32[]{:S(2)}, u32[]{:S(2)}) collective-permute-start(f32[1,32,10]{1,0,2:T(1,128)S(1)} %get-tuple-element.561), channel_id=1, source_target_pairs={{4,0},{8,4},{12,8},{16,12},{20,16},{24,20},{28,24},{5,1},{9,5},{13... | collective-permute-start | bytes 3848 | tf_op jit(solution)/shard_map/ppermute | solution.py:28
  530.0 3.8 collective-permute-start.39
  534.0 9.6 %collective-permute-start.41 = (f32[10,1,10]{1,0,2:T(8,128)S(1)}, f32[10,1,10]{1,0,2:T(8,128)S(1)}, u32[]{:S(2)}, u32[]{:S(2)}) collective-permute-start(f32[10,1,10]{1,0,2:T(8,128)S(1)} %get-tuple-element.545), channel_id=1, source_target_pairs={{0,1},{1,2},{2,3},{4,5},{5,6},{6,7},{8,9},{9,10},{10,11},{12,13},{... | collective-permute-start | bytes 1208 | tf_op jit(solution)/shard_map/ppermute | solution.py:26
  541.3 15.4 %collective-permute-start.40 = (f32[10,1,10]{1,0,2:T(8,128)S(1)}, f32[10,1,10]{1,0,2:T(8,128)S(1)}, u32[]{:S(2)}, u32[]{:S(2)}) collective-permute-start(f32[10,1,10]{1,0,2:T(8,128)S(1)} %get-tuple-element.544), channel_id=1, source_target_pairs={{1,0},{2,1},{3,2},{5,4},{6,5},{7,6},{9,8},{10,9},{11,10},{13,12},{... | collective-permute-start | bytes 1208 | tf_op jit(solution)/shard_map/ppermute | solution.py:28
  557.6 4.4 collective-permute-start.42
  560.7 4.4 collective-permute-start.43
  565.0 5.8 collective-permute-start.44
  568.9 3.1 collective-permute-start.45
  572.1 8.2 %collective-permute-start.47 = (f32[10,1,10]{1,0,2:T(8,128)S(1)}, f32[10,1,10]{1,0,2:T(8,128)S(1)}, u32[]{:S(2)}, u32[]{:S(2)}) collective-permute-start(f32[10,1,10]{1,0,2:T(8,128)S(1)} %get-tuple-element.543), channel_id=1, source_target_pairs={{0,1},{1,2},{2,3},{4,5},{5,6},{6,7},{8,9},{9,10},{10,11},{12,13},{... | collective-permute-start | bytes 1208 | tf_op jit(solution)/shard_map/ppermute | solution.py:26
  578.7 12.1 %collective-permute-start.46 = (f32[10,1,10]{1,0,2:T(8,128)S(1)}, f32[10,1,10]{1,0,2:T(8,128)S(1)}, u32[]{:S(2)}, u32[]{:S(2)}) collective-permute-start(f32[10,1,10]{1,0,2:T(8,128)S(1)} %get-tuple-element.542), channel_id=1, source_target_pairs={{1,0},{2,1},{3,2},{5,4},{6,5},{7,6},{9,8},{10,9},{11,10},{13,12},{... | collective-permute-start | bytes 1208 | tf_op jit(solution)/shard_map/ppermute | solution.py:28
  590.9 3.4 collective-permute-start.48
  593.0 4.6 collective-permute-start.49
  597.6 9.5 %collective-permute-start.50 = (f32[1,32,10]{1,0,2:T(1,128)S(1)}, f32[1,32,10]{1,0,2:T(1,128)S(1)}, u32[]{:S(2)}, u32[]{:S(2)}) collective-permute-start(f32[1,32,10]{1,0,2:T(1,128)S(1)} %get-tuple-element.557), channel_id=1, source_target_pairs={{4,0},{8,4},{12,8},{16,12},{20,16},{24,20},{28,24},{5,1},{9,5},{13... | collective-permute-start | bytes 3848 | tf_op jit(solution)/shard_map/ppermute | solution.py:28
  603.9 3.9 collective-permute-start.51
  608.0 4.9 collective-permute-start.53
  610.8 13.1 %collective-permute-start.52 = (f32[10,1,10]{1,0,2:T(8,128)S(1)}, f32[10,1,10]{1,0,2:T(8,128)S(1)}, u32[]{:S(2)}, u32[]{:S(2)}) collective-permute-start(f32[10,1,10]{1,0,2:T(8,128)S(1)} %get-tuple-element.540), channel_id=1, source_target_pairs={{1,0},{2,1},{3,2},{5,4},{6,5},{7,6},{9,8},{10,9},{11,10},{13,12},{... | collective-permute-start | bytes 1208 | tf_op jit(solution)/shard_map/ppermute | solution.py:28
  624.0 5.1 collective-permute-start.54
  627.7 4.8 collective-permute-start.55
  632.5 7.3 %collective-permute-start.56 = (f32[1,32,10]{1,0,2:T(1,128)S(1)}, f32[1,32,10]{1,0,2:T(1,128)S(1)}, u32[]{:S(2)}, u32[]{:S(2)}) collective-permute-start(f32[1,32,10]{1,0,2:T(1,128)S(1)} %get-tuple-element.555), channel_id=1, source_target_pairs={{4,0},{8,4},{12,8},{16,12},{20,16},{24,20},{28,24},{5,1},{9,5},{13... | collective-permute-start | bytes 3848 | tf_op jit(solution)/shard_map/ppermute | solution.py:28
  636.0 4.5 collective-permute-start.57
  640.6 3.3 collective-permute-start.59
  641.9 13.6 %collective-permute-start.58 = (f32[10,1,10]{1,0,2:T(8,128)S(1)}, f32[10,1,10]{1,0,2:T(8,128)S(1)}, u32[]{:S(2)}, u32[]{:S(2)}) collective-permute-start(f32[10,1,10]{1,0,2:T(8,128)S(1)} %get-tuple-element.538), channel_id=1, source_target_pairs={{1,0},{2,1},{3,2},{5,4},{6,5},{7,6},{9,8},{10,9},{11,10},{13,12},{... | collective-permute-start | bytes 1208 | tf_op jit(solution)/shard_map/ppermute | solution.py:28
  (16 other events, 422.3 us)
Sparse Core Ops, SparseCore 0:
  433.1 83.2 reduce-scatter.1
where the time goes:
time: 671 us; the launch traced here: 663 us
  waiting for transfers between devices  228 us (34%)
  starting transfers between devices  190 us (28%)
  local copies, waits for them, and re-layouts  150 us (22%)
  other arithmetic  48.1 us (7%)
  blocking collectives  20.9 us (3%)
  between operations  15.1 us (2%)
  matrix products  10.6 us (2%)
    ppermute x28, waiting for transfers between devices, extended(): lax.ppermute(head, axis, [((i + 1) % count, i) for i in range(ends)])  120 us
    ppermute x28, starting transfers between devices, extended(): lax.ppermute(tail, axis, [(i, (i + 1) % count) for i in range(ends)])  110 us
    reduce_scatter x1, waiting for transfers between devices, body(): share = lax.psum_scatter(term, 'load', scatter_dimension=2, tiled=True)  83.4 us
    concatenate x4, local copies, waits for them, and re-layouts, apply_one_block(): values = jnp.concatenate(pieces, axis=0)  72.4 us
    ppermute x28, starting transfers between devices, extended(): lax.ppermute(head, axis, [((i + 1) % count, i) for i in range(ends)])  66.4 us
    while x64, local copies, waits for them, and re-layouts  38.8 us
    all_gather x1, blocking collectives, body(): lax.all_gather(chebyshev(density, brick_extend), 'load', axis=2, tiled=True)  20.9 us
    scatter-add x1, other arithmetic, body(): flat_force = jnp.zeros((3, rows * wide * depth), jnp.float32).at[:, local...  18.3 us
  transfers between devices with their start and end apart: 61, of which 36 were waited for; matrix products, arithmetic and copies ran while one was open for 8% of the time, Pallas kernels for 0%

commit v1 on v0

v1 whole, which is shorter than its diff:
```python
import functools

import jax
import jax.numpy as jnp
from jax import lax
from jax.experimental import pallas as pl
from jax.experimental.pallas import tpu as pltpu
from jax.sharding import PartitionSpec as P

SWEEPS = 4
JACOBI = 2

poisson_ratio = 0.3
filter_weight = 3.0
relax_factor = 0.6
modulus_floor = 0.05
lame = poisson_ratio / ((1 + poisson_ratio) * (1 - 2 * poisson_ratio))
shear = 1.0 / (2 * (1 + poisson_ratio))

R = 8
W = 32
A = 128
N = 3 * R * W
ROWS = 13
PITCH = 48
USED = 40
BLOCKS = USED // 8
CHUNK = 512
MESH = pl.DeviceIdType.MESH
AROUND = [(0, -1), (0, 1), (-1, -1), (-1, 1), (1, -1), (1, 1), (-1, 0), (1, 0)]


def chebyshev_factors():
    theta = 1.0 + 6.0 * filter_weight
    delta = 6.0 * filter_weight
    sigma = theta / delta
    ratio = 1.0 / sigma
    steps = []
    for _ in range(SWEEPS):
        following = 1.0 / (2.0 * sigma - ratio)
        steps.append((following * ratio, 2.0 * following / delta))
        ratio = following
    return theta, steps


def lanes(shape):
    return lax.broadcasted_iota(jnp.int32, shape, len(shape) - 1)


def lane_up(x):
    return jnp.where(lanes(x.shape) == A - 1, 0.0, pltpu.roll(x, A - 1, x.ndim - 1))


def lane_down(x):
    return jnp.where(lanes(x.shape) == 0, 0.0, pltpu.roll(x, 1, x.ndim - 1))


def turned(x, steps):
    steps %= A
    return pltpu.roll(x, steps, 1) if steps else x


def edge_pack(halves):
    lane = lanes(halves[0].shape)
    packed = jnp.zeros(halves[0].shape, jnp.float32)
    for row in range(R):
        at = W * (row % 4)
        for start, column in ((8 * row, 0), (64 + 8 * row, W - 8)):
            moved = turned(halves[row // 4], start - at - column)
            packed = jnp.where((lane >= start) & (lane < start + 8), moved, packed)
    return packed


def total(values):
    result = values[0]
    for value in values[1:]:
        result = result + value
    return result


def groups():
    return [
        ([(0, 1, 0, 0), (1, 0, 1, 0), (2, 0, 0, 1)], lame / 16, 2 * shear / 16),
        ([(0, 0, 1, 0), (1, 1, 0, 0)], shear / 16, None),
        ([(0, 0, 0, 1), (2, 1, 0, 0)], shear / 16, None),
        ([(1, 0, 0, 1), (2, 0, 1, 0)], shear / 16, None),
        ([(0, 0, 1, 1), (1, 1, 0, 1), (2, 1, 1, 0)], shear / 48, shear / 48),
        ([(0, 1, 0, 1), (1, 0, 1, 1)], lame / 48, 3 * shear / 48),
        ([(0, 1, 1, 0), (2, 0, 1, 1)], lame / 48, 3 * shear / 48),
        ([(1, 1, 1, 0), (2, 1, 0, 1)], lame / 48, 3 * shear / 48),
        ([(0, 1, 1, 1)], None, (lame + 4 * shear) / 144),
        ([(1, 1, 1, 1)], None, (lame + 4 * shear) / 144),
        ([(2, 1, 1, 1)], None, (lame + 4 * shear) / 144),
    ]


def element_forces(coefs, modulus):
    scaled = {}

    def times(weight, value):
        if weight not in scaled:
            scaled[weight] = modulus * weight
        return scaled[weight] * value

    forces = {}
    for members, joint, single in groups():
        if joint is not None:
            common = total([coefs[m] for m in members])
            if joint == single:
                for m in members:
                    forces[m] = times(joint, common + coefs[m])
                continue
            common = times(joint, common)
            for m in members:
                forces[m] = common if single is None else common + times(single, coefs[m])
        else:
            for m in members:
                forces[m] = times(single, coefs[m])
    return forces


def element_energy(coefs):
    terms = {}
    for members, joint, single in groups():
        if joint is not None:
            common = total([coefs[m] for m in members])
            terms.setdefault(joint, []).append(common * common)
        if single is not None:
            for m in members:
                terms.setdefault(single, []).append(coefs[m] * coefs[m])
    return total([weight * total(values) for weight, values in terms.items()])


def plane_sums(field, row, column):
    out = {}
    for c in range(3):
        near = field[c, row, pl.ds(column, 8), :]
        far = field[c, row, pl.ds(column + 1, 8), :]
        for q, value in ((0, near + far), (1, far - near)):
            up = lane_up(value)
            out[c, q, 0] = value + up
            out[c, q, 1] = up - value
    return out


KEYS = [(c, q, r) for c in range(3) for q in range(2) for r in range(2)]


def row_coefs(low, high):
    coefs = {}
    for c, q, r in KEYS:
        coefs[c, 0, q, r] = low[c, q, r] + high[c, q, r]
        coefs[c, 1, q, r] = high[c, q, r] - low[c, q, r]
    return coefs


def kernel(
    counts,
    depth,
    density,
    prior,
    support,
    load_nodes,
    load_forces,
    displacement,
    sensitivity,
    raw,
    own,
    tile,
    beside,
    packs,
    halo,
    halos,
    wave,
    wave2,
    remain,
    result,
    rows_low,
    rows_high,
    fixed_low,
    fixed_high,
    send_low,
    send_high,
    columns_low,
    columns_high,
    corners_low,
    corners_high,
    field,
    near_part,
    far_part,
    modulus,
    free,
    step_size,
    force,
    spread,
    energy,
    shares,
    weights,
    share,
    share_pack,
    beside2,
    packs2,
    ring_wave,
    ring_wave2,
    ring_remain,
    ring_result,
    around_send,
    around_recv,
    own_send,
    own_recv,
    halo_send,
    halo_recv,
    rows_send,
    rows_recv,
    column_send,
    column_recv,
    corner_send,
    corner_recv,
    share_send,
    share_recv,
    last_send,
    last_recv,
):
    n_load, n_x, n_y = counts
    wide = depth + 8
    load, gx, gy = lax.axis_index("load"), lax.axis_index("gx"), lax.axis_index("gy")

    def inside(dx, dy):
        return (gx + dx >= 0) & (gx + dx < n_x) & (gy + dy >= 0) & (gy + dy < n_y)

    def peer(step):
        return lax.rem(load + step, n_load)

    def each_peer(action):
        def one(step, carry):
            action(step)
            return carry

        lax.fori_loop(1, n_load, one, 0)

    def remote(src, dst, send, recv, where):
        return pltpu.make_async_remote_copy(
            src_ref=src,
            dst_ref=dst,
            send_sem=send,
            recv_sem=recv,
            device_id=where,
            device_id_type=MESH,
        )

    def toward(dx, dy):
        return (load, gx + dx, gy + dy)

    for index, (dx, dy) in enumerate(AROUND):

        @pl.when(jnp.logical_not(inside(dx, dy)))
        def _():
            if dy == 0:
                for ref in (beside, beside2):
                    ref[(dx + 1) // 2] = jnp.zeros(ref.shape[1:], jnp.float32)
            else:
                for ref in (packs, packs2):
                    ref[dx + 1, (dy + 1) // 2] = jnp.zeros(ref.shape[2:], jnp.float32)

    @pl.when(jnp.logical_not(inside(-1, 0)))
    def _():
        rows_low[...] = jnp.zeros(rows_low.shape, jnp.float32)
        fixed_low[...] = jnp.zeros(fixed_low.shape, jnp.int32)
        corners_low[0] = jnp.zeros(corners_low.shape[1:], jnp.float32)
        corners_high[0] = jnp.zeros(corners_high.shape[1:], jnp.float32)

    @pl.when(jnp.logical_not(inside(1, 0)))
    def _():
        rows_high[...] = jnp.zeros(rows_high.shape, jnp.float32)
        fixed_high[...] = jnp.zeros(fixed_high.shape, jnp.int32)
        corners_low[1] = jnp.zeros(corners_low.shape[1:], jnp.float32)
        corners_high[1] = jnp.zeros(corners_high.shape[1:], jnp.float32)

    @pl.when(jnp.logical_not(inside(0, -1)))
    def _():
        columns_low[...] = jnp.zeros(columns_low.shape, jnp.float32)

    @pl.when(jnp.logical_not(inside(0, 1)))
    def _():
        columns_high[...] = jnp.zeros(columns_high.shape, jnp.float32)

    barrier = pltpu.get_barrier_semaphore()
    each_peer(
        lambda step: pl.semaphore_signal(
            barrier, inc=1, device_id=(peer(step), gx, gy), device_id_type=MESH
        )
    )
    expected = n_load - 1
    for dx, dy in AROUND:
        expected = expected + inside(dx, dy).astype(jnp.int32)

        @pl.when(inside(dx, dy))
        def _():
            pl.semaphore_signal(
                barrier, inc=1, device_id=toward(dx, dy), device_id_type=MESH
            )

    for row in range(R):
        raw[row, :, 0:W] = density[row]
    halves = []
    for half in range(2):
        value = jnp.zeros((depth, A), jnp.float32)
        lane = lanes(value.shape)
        for row in range(4):
            moved = turned(raw[4 * half + row], W * row)
            value = jnp.where((lane >= W * row) & (lane < W * row + W), moved, value)
        halves.append(value)
        own[:, A * half : A * half + A] = value
        tile[load, :, A * half : A * half + A] = value
    own[:, 2 * A : 3 * A] = edge_pack(halves)

    for row in range(R):
        for c in range(3):
            send_low[11 * row + 3 * c : 11 * row + 3 * c + 3, :] = prior[0, c, row, 0:3, :]
            send_high[7 * row + 2 * c : 7 * row + 2 * c + 2, :] = prior[0, c, row, W - 2 : W, :]
        send_low[11 * row + 9 : 11 * row + 11, :] = support[row, 0:2, :].astype(jnp.float32)
        send_high[7 * row + 6 : 7 * row + 7, :] = support[row, W - 1 : W, :].astype(jnp.float32)

    pl.semaphore_wait(barrier, expected)

    def around(index, whole, narrow, send, recv, source, pack):
        dx, dy = AROUND[index]
        if dy == 0:
            return remote(
                source, whole.at[(1 - dx) // 2], send.at[index], recv.at[index], toward(dx, dy)
            )
        return remote(
            pack, narrow.at[1 - dx, (1 - dy) // 2], send.at[index], recv.at[index], toward(dx, dy)
        )

    first_around = [
        around(
            index,
            beside,
            packs,
            around_send,
            around_recv,
            own.at[:, pl.ds(0, 2 * A)],
            own.at[:, pl.ds(2 * A, A)],
        )
        for index in range(8)
    ]
    opposite = [AROUND.index((-dx, -dy)) for dx, dy in AROUND]

    for index, (dx, dy) in enumerate(AROUND):

        @pl.when(inside(dx, dy))
        def _():
            first_around[index].start()

    def own_copy(step):
        return remote(
            own.at[:, pl.ds(0, 2 * A)],
            tile.at[load],
            own_send.at[step],
            own_recv.at[step],
            (peer(step), gx, gy),
        )

    each_peer(lambda step: own_copy(step).start())

    row_copies = [
        (-1, remote(prior.at[0, :, pl.ds(0, 3)], rows_high, rows_send.at[0], rows_recv.at[0], toward(-1, 0))),
        (-1, remote(support.at[pl.ds(0, 2)], fixed_high, rows_send.at[1], rows_recv.at[1], toward(-1, 0))),
        (1, remote(prior.at[0, :, pl.ds(R - 2, 2)], rows_low, rows_send.at[2], rows_recv.at[2], toward(1, 0))),
        (1, remote(support.at[pl.ds(R - 1, 1)], fixed_low, rows_send.at[3], rows_recv.at[3], toward(1, 0))),
    ]
    column_copies = [
        (-1, remote(send_low, columns_high, column_send.at[0], column_recv.at[0], toward(0, -1))),
        (1, remote(send_high, columns_low, column_send.at[1], column_recv.at[1], toward(0, 1))),
    ]
    for dy, copy in column_copies:
        pl.when(inside(0, dy))(copy.start)
    for dx, copy in row_copies:
        pl.when(inside(dx, 0))(copy.start)

    flat = load_nodes[...]
    column_bits = (n_y * W).bit_length() - 1
    node_row = lax.shift_right_logical(flat, 7 + column_bits) - gx * R + 1
    node_column = (lax.shift_right_logical(flat, 7) & (n_y * W - 1)) - gy * W + 2
    held = (node_row >= 0) & (node_row < 11) & (node_column >= 0) & (node_column < USED)
    spread[0:1, :] = jnp.where(held, node_row * USED + node_column, -1)
    spread[1:2, :] = flat & (A - 1)
    force[...] = jnp.zeros(force.shape, jnp.float32)

    def add_loads(index, carry):
        span = pl.ds(pl.multiple_of(index * CHUNK, CHUNK), CHUNK)
        place = spread[0:1, span]
        depth_of = spread[1:2, span]
        left = jnp.where(
            lax.broadcasted_iota(jnp.int32, (11 * USED, CHUNK), 0) == place, 1.0, 0.0
        ).astype(jnp.bfloat16)
        here = lax.broadcasted_iota(jnp.int32, (A, CHUNK), 0) == depth_of
        rest = [load_forces[0, c : c + 1, span] for c in range(3)]
        for part in range(3):
            rights = []
            for c in range(3):
                rounded = rest[c].astype(jnp.bfloat16).astype(jnp.float32)
                rest[c] = rest[c] - rounded
                rights.append(jnp.where(here, rounded, 0.0).astype(jnp.bfloat16))
            force[...] += lax.dot_general(
                left,
                jnp.concatenate(rights, axis=0),
                (((1,), (1,)), ((), ())),
                preferred_element_type=jnp.float32,
            )
        return carry

    lax.fori_loop(0, load_nodes.shape[1] // CHUNK, add_loads, 0)

    for index, (dx, dy) in enumerate(AROUND):

        @pl.when(inside(dx, dy))
        def _():
            first_around[opposite[index]].wait_recv()

    lane = lanes((depth, A))
    halo[:, 0:A] = beside[0, :, A : 2 * A]
    halo[:, A : 2 * A] = beside[1, :, 0:A]
    halo[:, 2 * A : 3 * A] = jnp.where(lane < 64, beside[1, :, A : 2 * A], beside[0, :, 0:A])
    for index in range(3):
        at = (3 + index) * A
        halo[:, at : at + A] = jnp.where(lane < 64, packs[index, 1], packs[index, 0])
    halos[load] = halo[...]

    def halo_copy(step):
        return remote(
            halo, halos.at[load], halo_send.at[step], halo_recv.at[step], (peer(step), gx, gy)
        )

    each_peer(lambda step: halo_copy(step).start())

    for dy, copy in column_copies:
        other = column_copies[0][1] if dy == 1 else column_copies[1][1]
        pl.when(inside(0, dy))(other.wait_recv)
    corner_copies = []
    for dx in (-1, 1):
        for part, (source, target) in enumerate(
            ((columns_low, corners_low), (columns_high, corners_high))
        ):
            at = (dx + 1) + part
            corner_copies.append(
                (
                    dx,
                    remote(
                        source,
                        target.at[(1 - dx) // 2],
                        corner_send.at[at],
                        corner_recv.at[at],
                        toward(dx, 0),
                    ),
                )
            )
    for dx, copy in corner_copies:
        pl.when(inside(dx, 0))(copy.start)

    for ref in (wave, wave2, ring_wave, ring_wave2):

        def clear(row, carry):
            ref[row] = jnp.zeros(ref.shape[1:], jnp.float32)
            return carry

        lax.fori_loop(0, ref.shape[0], clear, 0)

    def clear_rows(row, carry):
        for c in range(3):
            field[c, row, W:PITCH, :] = jnp.zeros((PITCH - W, A), jnp.float32)
        free[row] = jnp.zeros((PITCH, A), jnp.float32)
        return carry

    lax.fori_loop(0, ROWS, clear_rows, 0)

    for c in range(3):
        for row in range(R):
            field[c, row + 2, 2 : 2 + W, :] = prior[0, c, row]
    for row in range(R):
        free[row + 2, 2 : 2 + W, :] = support[row].astype(jnp.float32)

    for dx, copy in row_copies + corner_copies:
        opposite_copy = {
            id(a[1]): b[1]
            for pairs in (
                (row_copies[0], row_copies[2]),
                (row_copies[1], row_copies[3]),
                (corner_copies[0], corner_copies[2]),
                (corner_copies[1], corner_copies[3]),
            )
            for a, b in (pairs, pairs[::-1])
        }[id(copy)]
        pl.when(inside(dx, 0))(opposite_copy.wait_recv)

    for c in range(3):
        for row in range(2):
            field[c, row, 2 : 2 + W, :] = rows_low[c, row]
        for row in range(3):
            field[c, row + 10, 2 : 2 + W, :] = rows_high[c, row]
    free[1, 2 : 2 + W, :] = fixed_low[0].astype(jnp.float32)
    for row in range(2):
        free[row + 10, 2 : 2 + W, :] = fixed_high[row].astype(jnp.float32)
    for row in range(-2, R + 3):
        if row < 0:
            low, high, at = corners_low.at[0], corners_high.at[0], row + R
        elif row < R:
            low, high, at = columns_low, columns_high, row
        else:
            low, high, at = corners_low.at[1], corners_high.at[1], row - R
        for c in range(3):
            field[c, row + 2, 0:2, :] = low[7 * at + 2 * c : 7 * at + 2 * c + 2, :]
            field[c, row + 2, 2 + W : 5 + W, :] = high[11 * at + 3 * c : 11 * at + 3 * c + 3, :]
        free[row + 2, 1:2, :] = low[7 * at + 6 : 7 * at + 7, :]
        free[row + 2, 2 + W : 4 + W, :] = high[11 * at + 9 : 11 * at + 11, :]

    def in_grid(row, columns):
        row, columns = row + gx * R, columns + gy * W
        return (row >= 0) & (row < n_x * R) & (columns >= 0) & (columns < n_y * W)

    def set_free(row, carry):
        columns = lax.broadcasted_iota(jnp.int32, (PITCH, A), 0) - 2
        kept = in_grid(row - 2, columns) & (columns >= -1) & (columns <= W + 1)
        free[row] = jnp.where(kept & (free[row] == 0.0), 1.0, 0.0)
        return carry

    lax.fori_loop(1, 12, set_free, 0)

    def place(block, pieces):
        value = block.T
        for start, rows, columns, row, column in pieces:
            part = value[start : start + rows * columns].reshape(rows, columns, A)
            wave[row + 8 : row + 8 + rows, column + 16 : column + 16 + columns, :] = part

    each_peer(lambda step: own_copy(step).wait_recv())
    for half in range(2):
        place(tile[:, :, A * half : A * half + A].reshape(A, A), [(0, 4, W, 4 * half, 0)])
    each_peer(lambda step: halo_copy(step).wait_recv())
    layout = [
        [(0, 4, W, -4, 0)],
        [(0, 4, W, 8, 0)],
        [(0, 2, W, 12, 0), (64, 2, W, -6, 0)],
    ] + [[(0, 8, 8, dx * R, W), (64, 8, 8, dx * R, -8)] for dx in (-1, 0, 1)]
    for index, pieces in enumerate(layout):
        place(halos[:, :, A * index : A * index + A].reshape(A, A), pieces)

    theta, factors = chebyshev_factors()

    def start_filter(row, carry):
        source = wave[row, 8:56, :]
        direction = source / theta
        remain[row] = source
        result[row] = direction
        wave[row, 8:56, :] = direction
        return carry

    lax.fori_loop(2, 22, start_filter, 0)
    source, target = wave, wave2
    for sweep, (keep, gain) in enumerate(factors):

        def one_row(row, carry, source=source, target=target, keep=keep, gain=gain):
            middle = source[row, 8:56, :]
            near = (
                source[row - 1, 8:56, :]
                + source[row + 1, 8:56, :]
                + source[row, 7:55, :]
                + source[row, 9:57, :]
                + lane_up(middle)
                + lane_down(middle)
            )
            left = remain[row] - ((1.0 + 6.0 * filter_weight) * middle - filter_weight * near)
            columns = lax.broadcasted_iota(jnp.int32, (48, A), 0) - 8
            direction = jnp.where(in_grid(row - 8, columns), keep * middle + gain * left, 0.0)
            remain[row] = left
            result[row] = result[row] + direction
            target[row, 8:56, :] = direction
            return carry

        lax.fori_loop(3 + sweep, 21 - sweep, one_row, 0)
        source, target = target, source

    def set_modulus(row, carry):
        filtered = result[row + 6, 6 : 6 + USED, :]
        columns = lax.broadcasted_iota(jnp.int32, (USED, A), 0) - 2
        modulus[row, 0:8, :] = jnp.zeros((8, A), jnp.float32)
        modulus[row, 8 : 8 + USED, :] = jnp.where(
            in_grid(row - 2, columns), modulus_floor + filtered * filtered, 0.0
        )
        return carry

    lax.fori_loop(0, 12, set_modulus, 0)
    for half in range(2):
        tall = result[8 + 4 * half : 12 + 4 * half, 8 : 8 + W, :].reshape(A, A)
        weights[4 : 4 + A, A * half : A * half + A] = tall.T
    weights[0:4, :] = jnp.zeros((4, 2 * A), jnp.float32)
    weights[4 + A : 8 + A, :] = jnp.zeros((4, 2 * A), jnp.float32)

    def set_step(row, carry):
        around_node = total(
            [modulus[row - 1 + p, 7 + q : 7 + q + USED, :] for p in range(2) for q in range(2)]
        )
        around_node = around_node + lane_down(around_node)
        step_size[row] = relax_factor / ((lame + 4 * shear) / 9 * around_node)
        return carry

    lax.fori_loop(1, 12, set_step, 0)

    for sweep in range(JACOBI):
        first, last = 1 + sweep, 12 - sweep
        for block in range(BLOCKS):

            def one_element_row(row, carry, column=8 * block):
                low, pending = carry
                low = dict(zip(KEYS, low))
                high = plane_sums(field, row + 1, column)
                forces = element_forces(
                    row_coefs(low, high), modulus[row, pl.ds(column + 8, 8), :]
                )
                node = {}
                following = []
                for at, (c, q, r) in enumerate(KEYS):
                    change = forces[c, 1, q, r]
                    if (c, 0, q, r) in forces:
                        same = forces[c, 0, q, r]
                        node[c, q, r] = pending[at] + (same - change)
                        following.append(same + change)
                    else:
                        node[c, q, r] = pending[at] - change
                        following.append(change)
                for c in range(3):
                    both = []
                    for q in range(2):
                        lower = node[c, q, 0] - node[c, q, 1]
                        upper = node[c, q, 0] + node[c, q, 1]
                        both.append(lower + lane_down(upper))
                    near_part[c, row, pl.ds(column, 8), :] = both[0] - both[1]
                    far_part[c, row, pl.ds(column + 1, 8), :] = both[0] + both[1]
                return [high[key] for key in KEYS], following

            low = plane_sums(field, first - 1, 8 * block)
            nothing = [jnp.zeros((8, A), jnp.float32)] * len(KEYS)
            lax.fori_loop(
                first - 1, last, one_element_row, ([low[key] for key in KEYS], nothing)
            )

        def one_node_row(row, carry):
            for block in range(BLOCKS):
                span = pl.ds(8 * block, 8)
                rate = step_size[row, span, :]
                open_here = free[row, span, :] > 0.0
                for c in range(3):
                    applied = near_part[c, row, span, :] + far_part[c, row, span, :]
                    load_here = force[pl.ds(pl.multiple_of((row - 1) * USED + 8 * block, 8), 8), A * c : A * c + A]
                    moved = field[c, row, span, :] + (load_here - applied) * rate
                    field[c, row, span, :] = jnp.where(open_here, moved, 0.0)
            return carry

        lax.fori_loop(first, last, one_node_row, 0)

    for block in range(W // 8):

        def one_energy_row(row, low, column=8 * block + 2):
            high = plane_sums(field, row + 1, column)
            value = element_energy(row_coefs(dict(zip(KEYS, low)), high))
            remain[row, pl.ds(column - 2, 8), :] = value
            return [high[key] for key in KEYS]

        low = plane_sums(field, 2, 8 * block + 2)
        lax.fori_loop(2, 10, one_energy_row, [low[key] for key in KEYS])
    for half in range(2):
        tall = remain[2 + 4 * half : 6 + 4 * half, 0:W, :].reshape(A, A)
        energy[4 : 4 + A, A * half : A * half + A] = tall.T
    energy[0:4, :] = jnp.zeros((4, 2 * A), jnp.float32)
    energy[4 + A : 8 + A, :] = jnp.zeros((4, 2 * A), jnp.float32)

    for c in range(3):
        for row in range(R):
            displacement[0, c, row] = field[c, row + 2, 2 : 2 + W, :]

    def slab(owner):
        return pl.ds(pl.multiple_of(owner * depth, 8), wide)

    def share_copy(step):
        return remote(
            energy.at[slab(peer(step)), :],
            shares.at[load],
            share_send.at[step],
            share_recv.at[step],
            (peer(step), gx, gy),
        )

    each_peer(lambda step: share_copy(step).start())
    shares[load] = energy[slab(load), :]
    each_peer(lambda step: share_copy(step).wait_recv())
    summed = total([shares[index] for index in range(n_load)])
    value = -(2.0 / n_load) * weights[slab(load), :] * summed
    share[...] = value
    share_pack[...] = edge_pack([value[:, 0:A], value[:, A : 2 * A]])

    last_around = [
        around(index, beside2, packs2, last_send, last_recv, share, share_pack)
        for index in range(8)
    ]
    for index, (dx, dy) in enumerate(AROUND):

        @pl.when(inside(dx, dy))
        def _():
            last_around[index].start()

    for index, (dx, dy) in enumerate(AROUND):

        @pl.when(inside(dx, dy))
        def _():
            last_around[opposite[index]].wait_recv()

    lane = lanes((wide, A))
    for row in range(-4, R + 4):
        if row < 0:
            body, pack = beside2[0, :, A : 2 * A], 0
        elif row < R:
            body, pack = share[:, A * (row // 4) : A * (row // 4) + A], 1
        else:
            body, pack = beside2[1, :, 0:A], 2
        at = row % R
        line = turned(body, 4 - W * (at % 4))
        after = turned(packs2[pack, 1], 4 + W - 8 * at)
        before = turned(packs2[pack, 0], -4 - 64 - 8 * at)
        line = jnp.where(lane < 4, before, line)
        line = jnp.where(lane >= W + 4, after, line)
        line = jnp.where(lane < W + 8, line, 0.0)
        direction = line / theta
        ring_remain[row + 4] = line
        ring_result[row + 4] = direction
        ring_wave[row + 4, 8 : 8 + wide, :] = direction

    source, target = ring_wave, ring_wave2
    for sweep, (keep, gain) in enumerate(factors):

        def one_ring_row(row, carry, source=source, target=target, keep=keep, gain=gain):
            middle = source[row, 8 : 8 + wide, :]
            near = (
                source[row - 1, 8 : 8 + wide, :]
                + source[row + 1, 8 : 8 + wide, :]
                + source[row, 7 : 7 + wide, :]
                + source[row, 9 : 9 + wide, :]
                + pltpu.roll(middle, A - 1, 1)
                + pltpu.roll(middle, 1, 1)
            )
            left = ring_remain[row] - (
                (1.0 + 6.0 * filter_weight) * middle - filter_weight * near
            )
            layer = lax.broadcasted_iota(jnp.int32, (wide, A), 0) - 4 + load * depth
            kept = in_grid(row - 4, lane - 4) & (layer >= 0) & (layer < A) & (lane < W + 8)
            direction = jnp.where(kept, keep * middle + gain * left, 0.0)
            ring_remain[row] = left
            ring_result[row] = ring_result[row] + direction
            target[row, 8 : 8 + wide, :] = direction
            return carry

        lax.fori_loop(1 + sweep, 15 - sweep, one_ring_row, 0)
        source, target = target, source
    for row in range(R):
        moved = turned(ring_result[row + 4], -4)
        raw[row] = moved[4 : 4 + depth]
        sensitivity[row] = raw[row, :, 0:W]

    for index, (dx, dy) in enumerate(AROUND):

        @pl.when(inside(dx, dy))
        def _():
            first_around[index].wait_send()
            last_around[index].wait_send()

    for dx, copy in row_copies + corner_copies:
        pl.when(inside(dx, 0))(copy.wait_send)
    for dy, copy in column_copies:
        pl.when(inside(0, dy))(copy.wait_send)
    each_peer(lambda step: own_copy(step).wait_send())
    each_peer(lambda step: halo_copy(step).wait_send())
    each_peer(lambda step: share_copy(step).wait_send())


def body(counts, density, displacement_prior, support, load_nodes, load_forces):
    n_load = counts[0]
    depth = A // n_load
    wide = depth + 8
    picks = load_nodes.shape[1]
    real, whole = jnp.float32, jnp.int32
    scratch = [
        ((R, depth, A), real),
        ((depth, 3 * A), real),
        ((n_load, depth, 2 * A), real),
        ((2, depth, 2 * A), real),
        ((3, 2, depth, A), real),
        ((depth, 6 * A), real),
        ((n_load, depth, 6 * A), real),
        ((24, 64, A), real),
        ((24, 64, A), real),
        ((24, 48, A), real),
        ((24, 48, A), real),
        ((3, 2, W, A), real),
        ((3, 3, W, A), real),
        ((1, W, A), whole),
        ((2, W, A), whole),
        ((11 * R, A), real),
        ((7 * R, A), real),
        ((7 * R, A), real),
        ((11 * R, A), real),
        ((2, 7 * R, A), real),
        ((2, 11 * R, A), real),
        ((3, ROWS, PITCH, A), real),
        ((3, ROWS, PITCH, A), real),
        ((3, ROWS, PITCH, A), real),
        ((12, 8 + USED, A), real),
        ((ROWS, PITCH, A), real),
        ((12, USED, A), real),
        ((11 * USED, 3 * A), real),
        ((8, picks), whole),
        ((A + 8, 2 * A), real),
        ((n_load, wide, 2 * A), real),
        ((A + 8, 2 * A), real),
        ((wide, 2 * A), real),
        ((wide, A), real),
        ((2, wide, 2 * A), real),
        ((3, 2, wide, A), real),
        ((16, wide + 16, A), real),
        ((16, wide + 16, A), real),
        ((16, wide, A), real),
        ((16, wide, A), real),
    ]
    semaphores = [8, 8, n_load, n_load, n_load, n_load, 4, 4, 2, 2, 4, 4, n_load, n_load, 8, 8]
    displacement, sensitivity = pl.pallas_call(
        functools.partial(kernel, counts, depth),
        out_shape=(
            jax.ShapeDtypeStruct(displacement_prior.shape, real),
            jax.ShapeDtypeStruct((R, depth, W), real),
        ),
        in_specs=[pl.BlockSpec(memory_space=pltpu.VMEM)] * 5,
        out_specs=(pl.BlockSpec(memory_space=pltpu.VMEM),) * 2,
        scratch_shapes=[pltpu.VMEM(shape, kind) for shape, kind in scratch]
        + [pltpu.SemaphoreType.DMA((count,)) for count in semaphores],
        compiler_params=pltpu.CompilerParams(
            collective_id=0, has_side_effects=True, vmem_limit_bytes=48 << 20
        ),
        name="elasticity",
    )(
        jnp.transpose(density, (0, 2, 1)),
        displacement_prior,
        support,
        load_nodes,
        load_forces,
    )
    return displacement, jnp.transpose(sensitivity, (0, 2, 1))


def solution(mesh):
    counts = tuple(mesh.shape[axis] for axis in ("load", "gx", "gy"))
    return jax.shard_map(
        functools.partial(body, counts),
        mesh=mesh,
        in_specs=(
            P("gx", "gy", "load"),
            P("load", None, "gx", "gy", None),
            P("gx", "gy", None),
            P("load", None),
            P("load", None, None),
        ),
        out_specs=(P("load", None, "gx", "gy", None), P("gx", "gy", "load")),
        check_vma=False,
    )
```

time: 671 us -> 80.7 us (0.12); the launches traced: 663 us -> 80.4 us
  waiting for transfers between devices: 228 us -> 0 us
  starting transfers between devices: 190 us -> 0 us
  local copies, waits for them, and re-layouts: 150 us -> 4.03 us
  Pallas kernels: 0 us -> 75.7 us
  other arithmetic: 48.1 us -> 0 us
  blocking collectives: 20.9 us -> 0 us
  between operations: 15.1 us -> 0.68 us
  matrix products: 10.6 us -> 0 us
    ppermute x60 -> x0, starting transfers between devices: 190 us -> none  [the longest x28 110 us: extended(): lax.ppermute(tail, axis, [(i, (i + 1) % count) for i in range(ends)])]
    ppermute x60 -> x0, waiting for transfers between devices: 145 us -> none  [the longest x28 120 us: extended(): lax.ppermute(head, axis, [((i + 1) % count, i) for i in range(ends)])]
    concatenate x9 -> x0, local copies, waits for them, and re-layouts: 87.5 us -> none  [the longest x4 72.4 us: apply_one_block(): values = jnp.concatenate(pieces, axis=0)]
    reduce_scatter x1 -> x0, waiting for transfers between devices: 83.4 us -> none  [body(): share = lax.psum_scatter(term, 'load', scatter_dimension=2, tiled=True)]
    pallas_call x0 -> x1, Pallas kernels: none -> 75.7 us  [body(): pl.pallas_call(functools.partial(kernel, counts, depth), out_shape=(jax.S...]
    while x64 -> x0, local copies, waits for them, and re-layouts: 38.8 us -> none
    all_gather x1 -> x0, blocking collectives: 20.9 us -> none  [body(): lax.all_gather(chebyshev(density, brick_extend), 'load', axis=2, tiled=True)]
    scatter-add x1 -> x0, other arithmetic: 18.3 us -> none  [body(): flat_force = jnp.zeros((3, rows * wide * depth), jnp.float32).at[:, local...]
  transfers between devices with their start and end apart: 61 -> 0, of which waited for: 36 -> 0; matrix products, arithmetic and copies ran while one was open for 8% -> 0% of each run, Pallas kernels for 0% -> 0%
where the time goes in v1:
time: 80.7 us; the launch traced here: 80.4 us
  Pallas kernels  75.7 us (94%)
  local copies, waits for them, and re-layouts  4.03 us (5%)
    pallas_call x1, Pallas kernels, body(): pl.pallas_call(functools.partial(kernel, counts, depth), out_shape=(jax.S...  75.7 us
    unnamed x11, local copies, waits for them, and re-layouts  4.03 us

profile of v1, /device:TPU:1, one launch (start us, length us, event | category | flops | bytes accessed | tf_op | source)
XLA Modules:
  0.0 80.4 jit_solution(15951631672950449561)
XLA Ops:
  0.6 0.0 copy-start.2
  0.6 0.0 copy-start.3
  0.6 0.8 copy.7.load_forces
  1.4 0.0 copy-done.2
  1.4 0.0 copy-done.3
  1.4 0.0 copy-start
  1.4 1.0 %copy-done = f32[1,3,8,32,128]{4,3,2,1,0:T(8,128)S(1)} copy-done((f32[1,3,8,32,128]{4,3,2,1,0:T(8,128)S(1)}, f32[1,3,8,32,128]{4,3,2,1,0:T(8,128)}, u32[]{:S(2)}) %copy-start) | copy-done | bytes 393240
  2.4 0.0 copy-start.1
  2.4 0.9 %copy-done.1 = s32[8,32,128]{2,1,0:T(8,128)S(1)} copy-done((s32[8,32,128]{2,1,0:T(8,128)S(1)}, s32[8,32,128]{2,1,0:T(8,128)}, u32[]{:S(2)}) %copy-start.1) | copy-done | bytes 131096
  3.3 75.7 %elasticity.1 = (f32[1,3,8,32,128]{4,3,2,1,0:T(8,128)S(1)}, f32[8,8,32]{2,1,0:T(8,128)S(1)}) custom-call(f32[8,8,32]{2,1,0:T(8,128)S(1)} %bitcast.2, f32[1,3,8,32,128]{4,3,2,1,0:T(8,128)S(1)} %copy-done, s32[8,32,128]{2,1,0:T(8,128)S(1)} %copy-done.1, s32[1,2048]{1,0:T(1,128)S(1)} %copy-done.3, f32[1,3,2048]{2,1,0:T(4,128)S(1)} %copy.7.load_forces), custom_call_target="tpu_custom_call" | custom-call | tf_op jit(solution)/shard_map/elasticity/pallas_call | solution.py:833
  79.1 0.7 copy.10
  79.8 0.6 copy.11
Async XLA Ops:
  0.6 0.8 copy-start.2
  0.6 0.8 copy-start.3
  1.4 1.0 %copy-start = (f32[1,3,8,32,128]{4,3,2,1,0:T(8,128)S(1)}, f32[1,3,8,32,128]{4,3,2,1,0:T(8,128)}, u32[]{:S(2)}) copy-start(f32[1,3,8,32,128]{4,3,2,1,0:T(8,128)} %prior.1) | copy-start | bytes 1179652
  2.4 0.9 %copy-start.1 = (s32[8,32,128]{2,1,0:T(8,128)S(1)}, s32[8,32,128]{2,1,0:T(8,128)}, u32[]{:S(2)}) copy-start(s32[8,32,128]{2,1,0:T(8,128)} %support.1) | copy-start | bytes 393220

commit v2 on v1

--- a/solution.py
+++ b/solution.py
@@ -131,16 +131,33 @@
     return total([weight * total(values) for weight, values in terms.items()])
 
 
-def plane_sums(field, row, column):
+def plane_sums(field, lifted, row, column):
     out = {}
     for c in range(3):
         near = field[c, row, pl.ds(column, 8), :]
         far = field[c, row, pl.ds(column + 1, 8), :]
-        for q, value in ((0, near + far), (1, far - near)):
-            up = lane_up(value)
+        near_up = lifted[c, row, pl.ds(column, 8), :]
+        far_up = lifted[c, row, pl.ds(column + 1, 8), :]
+        for q, value, up in ((0, near + far, near_up + far_up), (1, far - near, far_up - near_up)):
             out[c, q, 0] = value + up
             out[c, q, 1] = up - value
     return out
+
+
+def in_groups(first, last, size, action, carry=0):
+    trips = (last - first) // size
+
+    def trip(index, carry):
+        for at in range(size):
+            carry = action(first + index * size + at, carry)
+        return carry
+
+    if trips > 1:
+        carry = lax.fori_loop(0, trips, trip, carry)
+        first += trips * size
+    for row in range(first, last):
+        carry = action(row, carry)
+    return carry
 
 
 KEYS = [(c, q, r) for c in range(3) for q in range(2) for r in range(2)]
@@ -157,13 +174,18 @@
 def kernel(
     counts,
     depth,
+    density_in,
+    prior_in,
+    support_in,
+    nodes_in,
+    forces_in,
+    displacement,
+    sensitivity,
     density,
     prior,
     support,
     load_nodes,
     load_forces,
-    displacement,
-    sensitivity,
     raw,
     own,
     tile,
@@ -204,6 +226,11 @@
     ring_wave2,
     ring_remain,
     ring_result,
+    lifted,
+    near_upper,
+    far_upper,
+    mask,
+    ring_mask,
     around_send,
     around_recv,
     own_send,
@@ -220,6 +247,7 @@
     share_recv,
     last_send,
     last_recv,
+    fetched,
 ):
     n_load, n_x, n_y = counts
     wide = depth + 8
@@ -251,6 +279,21 @@
     def toward(dx, dy):
         return (load, gx + dx, gy + dy)
 
+    fetches = [
+        pltpu.make_async_copy(source, target, fetched.at[index])
+        for index, (source, target) in enumerate(
+            (
+                (density_in, density),
+                (prior_in, prior),
+                (support_in, support),
+                (nodes_in, load_nodes),
+                (forces_in, load_forces),
+            )
+        )
+    ]
+    for fetch in fetches:
+        fetch.start()
+
     for index, (dx, dy) in enumerate(AROUND):
 
         @pl.when(jnp.logical_not(inside(dx, dy)))
@@ -300,6 +343,7 @@
                 barrier, inc=1, device_id=toward(dx, dy), device_id_type=MESH
             )
 
+    fetches[0].wait()
     for row in range(R):
         raw[row, :, 0:W] = density[row]
     halves = []
@@ -314,6 +358,9 @@
         tile[load, :, A * half : A * half + A] = value
     own[:, 2 * A : 3 * A] = edge_pack(halves)
 
+    fetches[1].wait()
+    fetches[2].wait()
+
     for row in range(R):
         for c in range(3):
             send_low[11 * row + 3 * c : 11 * row + 3 * c + 3, :] = prior[0, c, row, 0:3, :]
@@ -365,10 +412,10 @@
     each_peer(lambda step: own_copy(step).start())
 
     row_copies = [
-        (-1, remote(prior.at[0, :, pl.ds(0, 3)], rows_high, rows_send.at[0], rows_recv.at[0], toward(-1, 0))),
-        (-1, remote(support.at[pl.ds(0, 2)], fixed_high, rows_send.at[1], rows_recv.at[1], toward(-1, 0))),
-        (1, remote(prior.at[0, :, pl.ds(R - 2, 2)], rows_low, rows_send.at[2], rows_recv.at[2], toward(1, 0))),
-        (1, remote(support.at[pl.ds(R - 1, 1)], fixed_low, rows_send.at[3], rows_recv.at[3], toward(1, 0))),
+        (-1, remote(prior_in.at[0, :, pl.ds(0, 3)], rows_high, rows_send.at[0], rows_recv.at[0], toward(-1, 0))),
+        (-1, remote(support_in.at[pl.ds(0, 2)], fixed_high, rows_send.at[1], rows_recv.at[1], toward(-1, 0))),
+        (1, remote(prior_in.at[0, :, pl.ds(R - 2, 2)], rows_low, rows_send.at[2], rows_recv.at[2], toward(1, 0))),
+        (1, remote(support_in.at[pl.ds(R - 1, 1)], fixed_low, rows_send.at[3], rows_recv.at[3], toward(1, 0))),
     ]
     column_copies = [
         (-1, remote(send_low, columns_high, column_send.at[0], column_recv.at[0], toward(0, -1))),
@@ -379,6 +426,28 @@
     for dx, copy in row_copies:
         pl.when(inside(dx, 0))(copy.start)
 
+    def in_grid(row, columns):
+        row, columns = row + gx * R, columns + gy * W
+        return (row >= 0) & (row < n_x * R) & (columns >= 0) & (columns < n_y * W)
+
+    def set_mask(row, carry):
+        columns = lax.broadcasted_iota(jnp.int32, (48, A), 0) - 8
+        mask[row] = jnp.where(in_grid(row - 8, columns), 1.0, 0.0)
+        return carry
+
+    lax.fori_loop(3, 21, set_mask, 0)
+
+    def set_ring_mask(row, carry):
+        lane = lanes((wide, A))
+        layer = lax.broadcasted_iota(jnp.int32, (wide, A), 0) - 4 + load * depth
+        kept = in_grid(row - 4, lane - 4) & (layer >= 0) & (layer < A) & (lane < W + 8)
+        ring_mask[row] = jnp.where(kept, 1.0, 0.0)
+        return carry
+
+    lax.fori_loop(1, 15, set_ring_mask, 0)
+
+    fetches[3].wait()
+    fetches[4].wait()
     flat = load_nodes[...]
     column_bits = (n_y * W).bit_length() - 1
     node_row = lax.shift_right_logical(flat, 7 + column_bits) - gx * R + 1
@@ -396,7 +465,7 @@
             lax.broadcasted_iota(jnp.int32, (11 * USED, CHUNK), 0) == place, 1.0, 0.0
         ).astype(jnp.bfloat16)
         here = lax.broadcasted_iota(jnp.int32, (A, CHUNK), 0) == depth_of
-        rest = [load_forces[0, c : c + 1, span] for c in range(3)]
+        rest = [load_forces[c, :, span] for c in range(3)]
         for part in range(3):
             rights = []
             for c in range(3):
@@ -515,10 +584,6 @@
         free[row + 2, 1:2, :] = low[7 * at + 6 : 7 * at + 7, :]
         free[row + 2, 2 + W : 4 + W, :] = high[11 * at + 9 : 11 * at + 11, :]
 
-    def in_grid(row, columns):
-        row, columns = row + gx * R, columns + gy * W
-        return (row >= 0) & (row < n_x * R) & (columns >= 0) & (columns < n_y * W)
-
     def set_free(row, carry):
         columns = lax.broadcasted_iota(jnp.int32, (PITCH, A), 0) - 2
         kept = in_grid(row - 2, columns) & (columns >= -1) & (columns <= W + 1)
@@ -526,6 +591,13 @@
         return carry
 
     lax.fori_loop(1, 12, set_free, 0)
+
+    def lift(row, carry):
+        for c in range(3):
+            lifted[c, row] = lane_up(field[c, row])
+        return carry
+
+    lax.fori_loop(0, ROWS, lift, 0)
 
     def place(block, pieces):
         value = block.T
@@ -570,14 +642,13 @@
                 + lane_down(middle)
             )
             left = remain[row] - ((1.0 + 6.0 * filter_weight) * middle - filter_weight * near)
-            columns = lax.broadcasted_iota(jnp.int32, (48, A), 0) - 8
-            direction = jnp.where(in_grid(row - 8, columns), keep * middle + gain * left, 0.0)
+            direction = (keep * middle + gain * left) * mask[row]
             remain[row] = left
             result[row] = result[row] + direction
             target[row, 8:56, :] = direction
             return carry
 
-        lax.fori_loop(3 + sweep, 21 - sweep, one_row, 0)
+        in_groups(3 + sweep, 21 - sweep, 3, one_row)
         source, target = target, source
 
     def set_modulus(row, carry):
@@ -613,7 +684,7 @@
             def one_element_row(row, carry, column=8 * block):
                 low, pending = carry
                 low = dict(zip(KEYS, low))
-                high = plane_sums(field, row + 1, column)
+                high = plane_sums(field, lifted, row + 1, column)
                 forces = element_forces(
                     row_coefs(low, high), modulus[row, pl.ds(column + 8, 8), :]
                 )
@@ -629,45 +700,54 @@
                         node[c, q, r] = pending[at] - change
                         following.append(change)
                 for c in range(3):
-                    both = []
-                    for q in range(2):
-                        lower = node[c, q, 0] - node[c, q, 1]
-                        upper = node[c, q, 0] + node[c, q, 1]
-                        both.append(lower + lane_down(upper))
-                    near_part[c, row, pl.ds(column, 8), :] = both[0] - both[1]
-                    far_part[c, row, pl.ds(column + 1, 8), :] = both[0] + both[1]
+                    for sign, near_to, far_to in (
+                        (-1, near_part, far_part),
+                        (1, near_upper, far_upper),
+                    ):
+                        sums, changes = (
+                            node[c, q, 0] + node[c, q, 1] if sign > 0 else node[c, q, 0] - node[c, q, 1]
+                            for q in range(2)
+                        )
+                        near_to[c, row, pl.ds(column, 8), :] = sums - changes
+                        far_to[c, row, pl.ds(column + 1, 8), :] = sums + changes
                 return [high[key] for key in KEYS], following
 
-            low = plane_sums(field, first - 1, 8 * block)
+            low = plane_sums(field, lifted, first - 1, 8 * block)
             nothing = [jnp.zeros((8, A), jnp.float32)] * len(KEYS)
-            lax.fori_loop(
-                first - 1, last, one_element_row, ([low[key] for key in KEYS], nothing)
+            in_groups(
+                first - 1,
+                last,
+                (last - first + 1) // 2,
+                one_element_row,
+                ([low[key] for key in KEYS], nothing),
             )
 
         def one_node_row(row, carry):
-            for block in range(BLOCKS):
-                span = pl.ds(8 * block, 8)
-                rate = step_size[row, span, :]
-                open_here = free[row, span, :] > 0.0
-                for c in range(3):
-                    applied = near_part[c, row, span, :] + far_part[c, row, span, :]
-                    load_here = force[pl.ds(pl.multiple_of((row - 1) * USED + 8 * block, 8), 8), A * c : A * c + A]
-                    moved = field[c, row, span, :] + (load_here - applied) * rate
-                    field[c, row, span, :] = jnp.where(open_here, moved, 0.0)
+            span = pl.ds(0, USED)
+            rate = step_size[row]
+            open_here = free[row, span, :] > 0.0
+            for c in range(3):
+                applied = near_part[c, row, span, :] + far_part[c, row, span, :]
+                applied = applied + lane_down(near_upper[c, row, span, :] + far_upper[c, row, span, :])
+                load_here = force[pl.ds(pl.multiple_of((row - 1) * USED, 8), USED), A * c : A * c + A]
+                moved = field[c, row, span, :] + (load_here - applied) * rate
+                moved = jnp.where(open_here, moved, 0.0)
+                field[c, row, span, :] = moved
+                lifted[c, row, span, :] = lane_up(moved)
             return carry
 
-        lax.fori_loop(first, last, one_node_row, 0)
+        in_groups(first, last, 2, one_node_row)
 
     for block in range(W // 8):
 
         def one_energy_row(row, low, column=8 * block + 2):
-            high = plane_sums(field, row + 1, column)
+            high = plane_sums(field, lifted, row + 1, column)
             value = element_energy(row_coefs(dict(zip(KEYS, low)), high))
             remain[row, pl.ds(column - 2, 8), :] = value
             return [high[key] for key in KEYS]
 
-        low = plane_sums(field, 2, 8 * block + 2)
-        lax.fori_loop(2, 10, one_energy_row, [low[key] for key in KEYS])
+        low = plane_sums(field, lifted, 2, 8 * block + 2)
+        in_groups(2, 10, 4, one_energy_row, [low[key] for key in KEYS])
     for half in range(2):
         tall = remain[2 + 4 * half : 6 + 4 * half, 0:W, :].reshape(A, A)
         energy[4 : 4 + A, A * half : A * half + A] = tall.T
@@ -750,15 +830,13 @@
             left = ring_remain[row] - (
                 (1.0 + 6.0 * filter_weight) * middle - filter_weight * near
             )
-            layer = lax.broadcasted_iota(jnp.int32, (wide, A), 0) - 4 + load * depth
-            kept = in_grid(row - 4, lane - 4) & (layer >= 0) & (layer < A) & (lane < W + 8)
-            direction = jnp.where(kept, keep * middle + gain * left, 0.0)
+            direction = (keep * middle + gain * left) * ring_mask[row]
             ring_remain[row] = left
             ring_result[row] = ring_result[row] + direction
             target[row, 8 : 8 + wide, :] = direction
             return carry
 
-        lax.fori_loop(1 + sweep, 15 - sweep, one_ring_row, 0)
+        in_groups(1 + sweep, 15 - sweep, 14, one_ring_row)
         source, target = target, source
     for row in range(R):
         moved = turned(ring_result[row + 4], -4)
@@ -788,6 +866,11 @@
     picks = load_nodes.shape[1]
     real, whole = jnp.float32, jnp.int32
     scratch = [
+        ((R, depth, W), real),
+        (displacement_prior.shape, real),
+        ((R, W, A), whole),
+        ((1, picks), whole),
+        ((3, 1, picks), real),
         ((R, depth, A), real),
         ((depth, 3 * A), real),
         ((n_load, depth, 2 * A), real),
@@ -828,15 +911,20 @@
         ((16, wide + 16, A), real),
         ((16, wide, A), real),
         ((16, wide, A), real),
+        ((3, ROWS, PITCH, A), real),
+        ((3, ROWS, PITCH, A), real),
+        ((3, ROWS, PITCH, A), real),
+        ((24, 48, A), real),
+        ((16, wide, A), real),
     ]
-    semaphores = [8, 8, n_load, n_load, n_load, n_load, 4, 4, 2, 2, 4, 4, n_load, n_load, 8, 8]
+    semaphores = [8, 8, n_load, n_load, n_load, n_load, 4, 4, 2, 2, 4, 4, n_load, n_load, 8, 8, 5]
     displacement, sensitivity = pl.pallas_call(
         functools.partial(kernel, counts, depth),
         out_shape=(
             jax.ShapeDtypeStruct(displacement_prior.shape, real),
             jax.ShapeDtypeStruct((R, depth, W), real),
         ),
-        in_specs=[pl.BlockSpec(memory_space=pltpu.VMEM)] * 5,
+        in_specs=[pl.BlockSpec(memory_space=pltpu.HBM)] * 5,
         out_specs=(pl.BlockSpec(memory_space=pltpu.VMEM),) * 2,
         scratch_shapes=[pltpu.VMEM(shape, kind) for shape, kind in scratch]
         + [pltpu.SemaphoreType.DMA((count,)) for count in semaphores],
@@ -849,7 +937,7 @@
         displacement_prior,
         support,
         load_nodes,
-        load_forces,
+        jnp.transpose(load_forces, (1, 0, 2)),
     )
     return displacement, jnp.transpose(sensitivity, (0, 2, 1))
 

time: 80.7 us -> 59.2 us (0.73)
  Pallas kernels: 75.7 us -> 52.7 us
  local copies, waits for them, and re-layouts: 4.03 us -> 5.45 us
    pallas_call x1, Pallas kernels: 75.7 us -> 52.7 us  [body(): pl.pallas_call(functools.partial(kernel, counts, depth), out_shape=(jax.S...]
    unnamed x11 -> x12, local copies, waits for them, and re-layouts: 4.03 us -> 5.45 us
where the time goes in v2:
time: 59.2 us; the launch traced here: 58.8 us
  Pallas kernels  52.7 us (89%)
  local copies, waits for them, and re-layouts  5.45 us (9%)
  between operations  0.65 us (1%)
    pallas_call x1, Pallas kernels, body(): pl.pallas_call(functools.partial(kernel, counts, depth), out_shape=(jax.S...  52.7 us
    unnamed x12, local copies, waits for them, and re-layouts  5.45 us

profile of v2, /device:TPU:1, one launch (start us, length us, event | category | flops | bytes accessed | tf_op | source)
XLA Modules:
  0.0 58.8 jit_solution(8721292903588928448)
XLA Ops:
  0.6 0.0 copy-start
  0.6 1.0 %copy-done = f32[1,3,8,32,128]{4,3,2,1,0:T(8,128)S(1)} copy-done((f32[1,3,8,32,128]{4,3,2,1,0:T(8,128)S(1)}, f32[1,3,8,32,128]{4,3,2,1,0:T(8,128)}, u32[]{:S(2)}) %copy-start) | copy-done | bytes 393240
  1.6 0.0 copy-start.1
  1.6 0.9 %copy-done.1 = s32[8,32,128]{2,1,0:T(8,128)S(1)} copy-done((s32[8,32,128]{2,1,0:T(8,128)S(1)}, s32[8,32,128]{2,1,0:T(8,128)}, u32[]{:S(2)}) %copy-start.1) | copy-done | bytes 131096
  2.5 0.0 copy-start.2
  2.5 0.8 %copy-done.2 = f32[8,32,8]{1,2,0:T(8,128)S(1)} copy-done((f32[8,32,8]{1,2,0:T(8,128)S(1)}, f32[8,32,8]{1,2,0:T(8,128)}, u32[]{:S(2)}) %copy-start.2) | copy-done | bytes 8216
  3.3 0.0 copy-start.3
  3.3 0.7 %copy-done.3 = f32[1,3,2048]{2,0,1:T(1,128)S(1)} copy-done((f32[1,3,2048]{2,0,1:T(1,128)S(1)}, f32[1,3,2048]{2,0,1:T(1,128)}, u32[]{:S(2)}) %copy-start.3) | copy-done | bytes 24600
  4.0 0.0 copy-start.4
  4.0 0.7 %copy-done.4 = s32[1,2048]{1,0:T(1,128)S(1)} copy-done((s32[1,2048]{1,0:T(1,128)S(1)}, s32[1,2048]{1,0:T(1,128)}, u32[]{:S(2)}) %copy-start.4) | copy-done | bytes 8216
  4.7 52.7 %elasticity.1 = (f32[1,3,8,32,128]{4,3,2,1,0:T(8,128)S(1)}, f32[8,8,32]{2,1,0:T(8,128)S(1)}) custom-call(f32[8,8,32]{2,1,0:T(8,128)S(1)} %bitcast.3, f32[1,3,8,32,128]{4,3,2,1,0:T(8,128)S(1)} %copy-done, s32[8,32,128]{2,1,0:T(8,128)S(1)} %copy-done.1, s32[1,2048]{1,0:T(1,128)S(1)} %copy-done.4, f32[3,1,2048]{2,1,0:T(1,128)S(1)} %bitcast.5), custom_call_target="tpu_custom_call" | custom-call | tf_op jit(solution)/shard_map/elasticity/pallas_call | solution.py:921
  57.5 0.7 %copy.9 = f32[1,3,8,32,128]{4,3,2,1,0:T(8,128)} copy(f32[1,3,8,32,128]{4,3,2,1,0:T(8,128)S(1)} %get-tuple-element.8) | data formatting | bytes 786432
  58.2 0.6 %copy.10 = f32[8,32,8]{1,2,0:T(8,128)} copy(f32[8,32,8]{1,2,0:T(8,128)S(1)} %bitcast.4) | data formatting | bytes 16384
Async XLA Ops:
  0.6 1.0 %copy-start = (f32[1,3,8,32,128]{4,3,2,1,0:T(8,128)S(1)}, f32[1,3,8,32,128]{4,3,2,1,0:T(8,128)}, u32[]{:S(2)}) copy-start(f32[1,3,8,32,128]{4,3,2,1,0:T(8,128)} %prior_in.1) | copy-start | bytes 1179652
  1.6 0.9 %copy-start.1 = (s32[8,32,128]{2,1,0:T(8,128)S(1)}, s32[8,32,128]{2,1,0:T(8,128)}, u32[]{:S(2)}) copy-start(s32[8,32,128]{2,1,0:T(8,128)} %support_in.1) | copy-start | bytes 393220
  2.5 0.8 %copy-start.2 = (f32[8,32,8]{1,2,0:T(8,128)S(1)}, f32[8,32,8]{1,2,0:T(8,128)}, u32[]{:S(2)}) copy-start(f32[8,32,8]{1,2,0:T(8,128)} %param.5) | copy-start | bytes 24580
  3.3 0.7 %copy-start.3 = (f32[1,3,2048]{2,0,1:T(1,128)S(1)}, f32[1,3,2048]{2,0,1:T(1,128)}, u32[]{:S(2)}) copy-start(f32[1,3,2048]{2,0,1:T(1,128)} %param.9) | copy-start | bytes 73732
  4.0 0.7 %copy-start.4 = (s32[1,2048]{1,0:T(1,128)S(1)}, s32[1,2048]{1,0:T(1,128)}, u32[]{:S(2)}) copy-start(s32[1,2048]{1,0:T(1,128)} %nodes_in.1) | copy-start | bytes 24580

commit v3 on v2

--- a/solution.py
+++ b/solution.py
@@ -43,6 +43,22 @@
     return theta, steps
 
 
+def chebyshev_terms():
+    theta, steps = chebyshev_factors()
+    terms = []
+    before = None
+    for keep, gain in steps:
+        own, last = keep - gain * theta, 0.0
+        if before is None:
+            own += gain * theta
+        else:
+            own += gain / before[1]
+            last = -gain / before[1] * before[0]
+        terms.append((own, last, gain * filter_weight))
+        before = keep, gain
+    return theta, terms
+
+
 def lanes(shape):
     return lax.broadcasted_iota(jnp.int32, shape, len(shape) - 1)
 
@@ -53,6 +69,27 @@
 
 def lane_down(x):
     return jnp.where(lanes(x.shape) == 0, 0.0, pltpu.roll(x, 1, x.ndim - 1))
+
+
+def fold_pack(halves):
+    wide = halves[0].shape[0]
+    lane = lanes((wide, A))
+    packed = jnp.zeros((wide, A), jnp.float32)
+    for row in range(R):
+        at = W * (row % 4)
+        for start, column in ((4 * row, 0), (64 + 4 * row, W - 4)):
+            moved = turned(halves[row // 4], start - at - column)
+            packed = jnp.where((lane >= start) & (lane < start + 4), moved, packed)
+    if wide != 16:
+        return packed
+    lane = lanes((8, A))
+    return jnp.where((lane & 32) == 0, packed[0:8], turned(packed[8:16], 32))
+
+
+def unfolded(pack, steps):
+    if pack.shape[0] != 8:
+        return turned(pack, steps)
+    return jnp.concatenate([turned(pack, steps), turned(pack, steps - 32)], axis=0)
 
 
 def turned(x, steps):
@@ -69,6 +106,16 @@
             moved = turned(halves[row // 4], start - at - column)
             packed = jnp.where((lane >= start) & (lane < start + 8), moved, packed)
     return packed
+
+
+def peers_of(count):
+    side = 4 if count == 16 else count
+    steps = [(a, b) for a in range(count // side) for b in range(side)][1:]
+
+    def hops(step):
+        return min(step[0], count // side - step[0]) + min(step[1], side - step[1])
+
+    return side, sorted(steps, key=hops, reverse=True)
 
 
 def total(values):
@@ -193,8 +240,11 @@
     packs,
     halo,
     halos,
-    wave,
+    wave0,
+    wave1,
     wave2,
+    wave3,
+    wave4,
     remain,
     result,
     rows_low,
@@ -222,10 +272,11 @@
     share_pack,
     beside2,
     packs2,
-    ring_wave,
+    ring_wave0,
+    ring_wave1,
     ring_wave2,
-    ring_remain,
-    ring_result,
+    ring_wave3,
+    ring_wave4,
     lifted,
     near_upper,
     far_upper,
@@ -250,21 +301,25 @@
     fetched,
 ):
     n_load, n_x, n_y = counts
+    waves = [wave0, wave1, wave2, wave3, wave4]
+    wave = wave0
+    ring_waves = [ring_wave0, ring_wave1, ring_wave2, ring_wave3, ring_wave4]
     wide = depth + 8
     load, gx, gy = lax.axis_index("load"), lax.axis_index("gx"), lax.axis_index("gy")
 
     def inside(dx, dy):
         return (gx + dx >= 0) & (gx + dx < n_x) & (gy + dy >= 0) & (gy + dy < n_y)
 
+    side, steps = peers_of(n_load)
+
     def peer(step):
-        return lax.rem(load + step, n_load)
+        a, b = steps[step]
+        across = lax.rem(lax.div(load, side) + a, n_load // side)
+        return across * side + lax.rem(lax.rem(load, side) + b, side)
 
     def each_peer(action):
-        def one(step, carry):
+        for step in range(n_load - 1):
             action(step)
-            return carry
-
-        lax.fori_loop(1, n_load, one, 0)
 
     def remote(src, dst, send, recv, where):
         return pltpu.make_async_remote_copy(
@@ -370,11 +425,11 @@
 
     pl.semaphore_wait(barrier, expected)
 
-    def around(index, whole, narrow, send, recv, source, pack):
+    def around(index, whole, narrow, send, recv, sources, pack):
         dx, dy = AROUND[index]
         if dy == 0:
             return remote(
-                source, whole.at[(1 - dx) // 2], send.at[index], recv.at[index], toward(dx, dy)
+                sources[(1 + dx) // 2], whole.at[(1 - dx) // 2], send.at[index], recv.at[index], toward(dx, dy)
             )
         return remote(
             pack, narrow.at[1 - dx, (1 - dy) // 2], send.at[index], recv.at[index], toward(dx, dy)
@@ -387,7 +442,7 @@
             packs,
             around_send,
             around_recv,
-            own.at[:, pl.ds(0, 2 * A)],
+            [own.at[:, pl.ds(0, 2 * A)]] * 2,
             own.at[:, pl.ds(2 * A, A)],
         )
         for index in range(8)
@@ -445,6 +500,30 @@
         return carry
 
     lax.fori_loop(1, 15, set_ring_mask, 0)
+
+    def halo_copy(step, part):
+        span = pl.ds(part * 3 * A, 3 * A)
+        return remote(
+            halo.at[:, span],
+            halos.at[load, :, span],
+            halo_send.at[part, step],
+            halo_recv.at[part, step],
+            (peer(step), gx, gy),
+        )
+
+    for index, (dx, dy) in enumerate(AROUND):
+        if dy == 0:
+
+            @pl.when(inside(dx, dy))
+            def _():
+                first_around[opposite[index]].wait_recv()
+
+    lane = lanes((depth, A))
+    halo[:, 0:A] = beside[0, :, A : 2 * A]
+    halo[:, A : 2 * A] = beside[1, :, 0:A]
+    halo[:, 2 * A : 3 * A] = jnp.where(lane < 64, beside[1, :, A : 2 * A], beside[0, :, 0:A])
+    halos[load, :, 0 : 3 * A] = halo[:, 0 : 3 * A]
+    each_peer(lambda step: halo_copy(step, 0).start())
 
     fetches[3].wait()
     fetches[4].wait()
@@ -483,26 +562,17 @@
     lax.fori_loop(0, load_nodes.shape[1] // CHUNK, add_loads, 0)
 
     for index, (dx, dy) in enumerate(AROUND):
-
-        @pl.when(inside(dx, dy))
-        def _():
-            first_around[opposite[index]].wait_recv()
-
-    lane = lanes((depth, A))
-    halo[:, 0:A] = beside[0, :, A : 2 * A]
-    halo[:, A : 2 * A] = beside[1, :, 0:A]
-    halo[:, 2 * A : 3 * A] = jnp.where(lane < 64, beside[1, :, A : 2 * A], beside[0, :, 0:A])
+        if dy != 0:
+
+            @pl.when(inside(dx, dy))
+            def _():
+                first_around[opposite[index]].wait_recv()
+
     for index in range(3):
         at = (3 + index) * A
         halo[:, at : at + A] = jnp.where(lane < 64, packs[index, 1], packs[index, 0])
-    halos[load] = halo[...]
-
-    def halo_copy(step):
-        return remote(
-            halo, halos.at[load], halo_send.at[step], halo_recv.at[step], (peer(step), gx, gy)
-        )
-
-    each_peer(lambda step: halo_copy(step).start())
+        halos[load, :, at : at + A] = halo[:, at : at + A]
+    each_peer(lambda step: halo_copy(step, 1).start())
 
     for dy, copy in column_copies:
         other = column_copies[0][1] if dy == 1 else column_copies[1][1]
@@ -528,7 +598,7 @@
     for dx, copy in corner_copies:
         pl.when(inside(dx, 0))(copy.start)
 
-    for ref in (wave, wave2, ring_wave, ring_wave2):
+    for ref in waves[:4] + ring_waves[:4]:
 
         def clear(row, carry):
             ref[row] = jnp.zeros(ref.shape[1:], jnp.float32)
@@ -608,30 +678,26 @@
     each_peer(lambda step: own_copy(step).wait_recv())
     for half in range(2):
         place(tile[:, :, A * half : A * half + A].reshape(A, A), [(0, 4, W, 4 * half, 0)])
-    each_peer(lambda step: halo_copy(step).wait_recv())
     layout = [
         [(0, 4, W, -4, 0)],
         [(0, 4, W, 8, 0)],
         [(0, 2, W, 12, 0), (64, 2, W, -6, 0)],
     ] + [[(0, 8, 8, dx * R, W), (64, 8, 8, dx * R, -8)] for dx in (-1, 0, 1)]
     for index, pieces in enumerate(layout):
+        if index % 3 == 0:
+            each_peer(lambda step: halo_copy(step, index // 3).wait_recv())
         place(halos[:, :, A * index : A * index + A].reshape(A, A), pieces)
 
-    theta, factors = chebyshev_factors()
+    theta, terms = chebyshev_terms()
 
     def start_filter(row, carry):
-        source = wave[row, 8:56, :]
-        direction = source / theta
-        remain[row] = source
-        result[row] = direction
-        wave[row, 8:56, :] = direction
+        wave[row, 8:56, :] = wave[row, 8:56, :] / theta
         return carry
 
-    lax.fori_loop(2, 22, start_filter, 0)
-    source, target = wave, wave2
-    for sweep, (keep, gain) in enumerate(factors):
-
-        def one_row(row, carry, source=source, target=target, keep=keep, gain=gain):
+    in_groups(2, 22, 5, start_filter)
+    for sweep, (own_factor, last_factor, near_factor) in enumerate(terms):
+
+        def one_row(row, carry, source=waves[sweep], target=waves[sweep + 1]):
             middle = source[row, 8:56, :]
             near = (
                 source[row - 1, 8:56, :]
@@ -641,18 +707,17 @@
                 + lane_up(middle)
                 + lane_down(middle)
             )
-            left = remain[row] - ((1.0 + 6.0 * filter_weight) * middle - filter_weight * near)
-            direction = (keep * middle + gain * left) * mask[row]
-            remain[row] = left
-            result[row] = result[row] + direction
-            target[row, 8:56, :] = direction
+            direction = own_factor * middle + near_factor * near
+            if sweep:
+                direction = direction + last_factor * waves[sweep - 1][row, 8:56, :]
+            target[row, 8:56, :] = direction * mask[row]
             return carry
 
         in_groups(3 + sweep, 21 - sweep, 3, one_row)
-        source, target = target, source
 
     def set_modulus(row, carry):
-        filtered = result[row + 6, 6 : 6 + USED, :]
+        filtered = total([ref[row + 6, 14 : 14 + USED, :] for ref in waves])
+        result[row] = filtered
         columns = lax.broadcasted_iota(jnp.int32, (USED, A), 0) - 2
         modulus[row, 0:8, :] = jnp.zeros((8, A), jnp.float32)
         modulus[row, 8 : 8 + USED, :] = jnp.where(
@@ -660,9 +725,9 @@
         )
         return carry
 
-    lax.fori_loop(0, 12, set_modulus, 0)
+    in_groups(0, 12, 3, set_modulus)
     for half in range(2):
-        tall = result[8 + 4 * half : 12 + 4 * half, 8 : 8 + W, :].reshape(A, A)
+        tall = result[2 + 4 * half : 6 + 4 * half, 2 : 2 + W, :].reshape(A, A)
         weights[4 : 4 + A, A * half : A * half + A] = tall.T
     weights[0:4, :] = jnp.zeros((4, 2 * A), jnp.float32)
     weights[4 + A : 8 + A, :] = jnp.zeros((4, 2 * A), jnp.float32)
@@ -675,7 +740,7 @@
         step_size[row] = relax_factor / ((lame + 4 * shear) / 9 * around_node)
         return carry
 
-    lax.fori_loop(1, 12, set_step, 0)
+    in_groups(1, 12, 4, set_step)
 
     for sweep in range(JACOBI):
         first, last = 1 + sweep, 12 - sweep
@@ -756,7 +821,9 @@
 
     for c in range(3):
         for row in range(R):
-            displacement[0, c, row] = field[c, row + 2, 2 : 2 + W, :]
+            prior[0, c, row] = field[c, row + 2, 2 : 2 + W, :]
+    leave = pltpu.make_async_copy(prior, displacement, fetched.at[5])
+    leave.start()
 
     def slab(owner):
         return pl.ds(pl.multiple_of(owner * depth, 8), wide)
@@ -776,10 +843,11 @@
     summed = total([shares[index] for index in range(n_load)])
     value = -(2.0 / n_load) * weights[slab(load), :] * summed
     share[...] = value
-    share_pack[...] = edge_pack([value[:, 0:A], value[:, A : 2 * A]])
-
+    share_pack[...] = fold_pack([value[:, 0:A], value[:, A : 2 * A]])
+
+    sides = [share.at[:, pl.ds(0, A)], share.at[:, pl.ds(A, A)]]
     last_around = [
-        around(index, beside2, packs2, last_send, last_recv, share, share_pack)
+        around(index, beside2, packs2, last_send, last_recv, sides, share_pack)
         for index in range(8)
     ]
     for index, (dx, dy) in enumerate(AROUND):
@@ -797,52 +865,42 @@
     lane = lanes((wide, A))
     for row in range(-4, R + 4):
         if row < 0:
-            body, pack = beside2[0, :, A : 2 * A], 0
+            body, pack = beside2[0], 0
         elif row < R:
             body, pack = share[:, A * (row // 4) : A * (row // 4) + A], 1
         else:
-            body, pack = beside2[1, :, 0:A], 2
+            body, pack = beside2[1], 2
         at = row % R
         line = turned(body, 4 - W * (at % 4))
-        after = turned(packs2[pack, 1], 4 + W - 8 * at)
-        before = turned(packs2[pack, 0], -4 - 64 - 8 * at)
+        after = unfolded(packs2[pack, 1], 4 + W - 4 * at)
+        before = unfolded(packs2[pack, 0], -64 - 4 * at)
         line = jnp.where(lane < 4, before, line)
         line = jnp.where(lane >= W + 4, after, line)
         line = jnp.where(lane < W + 8, line, 0.0)
-        direction = line / theta
-        ring_remain[row + 4] = line
-        ring_result[row + 4] = direction
-        ring_wave[row + 4, 8 : 8 + wide, :] = direction
-
-    source, target = ring_wave, ring_wave2
-    for sweep, (keep, gain) in enumerate(factors):
-
-        def one_ring_row(row, carry, source=source, target=target, keep=keep, gain=gain):
-            middle = source[row, 8 : 8 + wide, :]
+        ring_waves[0][row + 4, 8 : 8 + wide, :] = line / theta
+
+    span = slice(8, 8 + wide)
+    for sweep, (own_factor, last_factor, near_factor) in enumerate(terms):
+        source = ring_waves[sweep]
+        for row in range(1 + sweep, 15 - sweep):
+            middle = source[row, span, :]
             near = (
-                source[row - 1, 8 : 8 + wide, :]
-                + source[row + 1, 8 : 8 + wide, :]
+                source[row - 1, span, :]
+                + source[row + 1, span, :]
                 + source[row, 7 : 7 + wide, :]
                 + source[row, 9 : 9 + wide, :]
                 + pltpu.roll(middle, A - 1, 1)
                 + pltpu.roll(middle, 1, 1)
             )
-            left = ring_remain[row] - (
-                (1.0 + 6.0 * filter_weight) * middle - filter_weight * near
-            )
-            direction = (keep * middle + gain * left) * ring_mask[row]
-            ring_remain[row] = left
-            ring_result[row] = ring_result[row] + direction
-            target[row, 8 : 8 + wide, :] = direction
-            return carry
-
-        in_groups(1 + sweep, 15 - sweep, 14, one_ring_row)
-        source, target = target, source
+            direction = own_factor * middle + near_factor * near
+            if sweep:
+                direction = direction + last_factor * ring_waves[sweep - 1][row, span, :]
+            ring_waves[sweep + 1][row, span, :] = direction * ring_mask[row]
     for row in range(R):
-        moved = turned(ring_result[row + 4], -4)
-        raw[row] = moved[4 : 4 + depth]
-        sensitivity[row] = raw[row, :, 0:W]
-
+        summed = total([ref[row + 4, 12 : 12 + depth, :] for ref in ring_waves])
+        sensitivity[row] = turned(summed, -4)[:, 0:W]
+
+    leave.wait()
     for index, (dx, dy) in enumerate(AROUND):
 
         @pl.when(inside(dx, dy))
@@ -855,7 +913,8 @@
     for dy, copy in column_copies:
         pl.when(inside(0, dy))(copy.wait_send)
     each_peer(lambda step: own_copy(step).wait_send())
-    each_peer(lambda step: halo_copy(step).wait_send())
+    each_peer(lambda step: halo_copy(step, 0).wait_send())
+    each_peer(lambda step: halo_copy(step, 1).wait_send())
     each_peer(lambda step: share_copy(step).wait_send())
 
 
@@ -863,6 +922,7 @@
     n_load = counts[0]
     depth = A // n_load
     wide = depth + 8
+    folded = 8 if wide == 16 else wide
     picks = load_nodes.shape[1]
     real, whole = jnp.float32, jnp.int32
     scratch = [
@@ -880,8 +940,11 @@
         ((n_load, depth, 6 * A), real),
         ((24, 64, A), real),
         ((24, 64, A), real),
+        ((24, 64, A), real),
+        ((24, 64, A), real),
+        ((24, 64, A), real),
         ((24, 48, A), real),
-        ((24, 48, A), real),
+        ((12, USED, A), real),
         ((3, 2, W, A), real),
         ((3, 3, W, A), real),
         ((1, W, A), whole),
@@ -904,20 +967,21 @@
         ((n_load, wide, 2 * A), real),
         ((A + 8, 2 * A), real),
         ((wide, 2 * A), real),
-        ((wide, A), real),
-        ((2, wide, 2 * A), real),
-        ((3, 2, wide, A), real),
+        ((folded, A), real),
+        ((2, wide, A), real),
+        ((3, 2, folded, A), real),
         ((16, wide + 16, A), real),
         ((16, wide + 16, A), real),
-        ((16, wide, A), real),
-        ((16, wide, A), real),
+        ((16, wide + 16, A), real),
+        ((16, wide + 16, A), real),
+        ((16, wide + 16, A), real),
         ((3, ROWS, PITCH, A), real),
         ((3, ROWS, PITCH, A), real),
         ((3, ROWS, PITCH, A), real),
         ((24, 48, A), real),
         ((16, wide, A), real),
     ]
-    semaphores = [8, 8, n_load, n_load, n_load, n_load, 4, 4, 2, 2, 4, 4, n_load, n_load, 8, 8, 5]
+    semaphores = [8, 8, n_load, n_load, (2, n_load), (2, n_load), 4, 4, 2, 2, 4, 4, n_load, n_load, 8, 8, 6]
     displacement, sensitivity = pl.pallas_call(
         functools.partial(kernel, counts, depth),
         out_shape=(
@@ -925,11 +989,11 @@
             jax.ShapeDtypeStruct((R, depth, W), real),
         ),
         in_specs=[pl.BlockSpec(memory_space=pltpu.HBM)] * 5,
-        out_specs=(pl.BlockSpec(memory_space=pltpu.VMEM),) * 2,
+        out_specs=(pl.BlockSpec(memory_space=pltpu.HBM), pl.BlockSpec(memory_space=pltpu.VMEM)),
         scratch_shapes=[pltpu.VMEM(shape, kind) for shape, kind in scratch]
-        + [pltpu.SemaphoreType.DMA((count,)) for count in semaphores],
+        + [pltpu.SemaphoreType.DMA(count if isinstance(count, tuple) else (count,)) for count in semaphores],
         compiler_params=pltpu.CompilerParams(
-            collective_id=0, has_side_effects=True, vmem_limit_bytes=48 << 20
+            collective_id=0, has_side_effects=True, vmem_limit_bytes=67_043_328
         ),
         name="elasticity",
     )(

time: 59.2 us -> 54.3 us (0.917)
  local copies, waits for them, and re-layouts: 5.45 us -> 2.39 us
  Pallas kernels: 52.7 us -> 51.1 us
    unnamed x12 -> x4, local copies, waits for them, and re-layouts: 5.45 us -> 2.39 us
    pallas_call x1, Pallas kernels: 52.7 us -> 51.1 us  [body(): pl.pallas_call(functools.partial(kernel, counts, depth), out_shape=(jax.S...]
where the time goes in v3:
time: 54.3 us; the launch traced here: 54.1 us
  Pallas kernels  51.1 us (94%)
  local copies, waits for them, and re-layouts  2.39 us (4%)
  between operations  0.65 us (1%)
    pallas_call x1, Pallas kernels, body(): pl.pallas_call(functools.partial(kernel, counts, depth), out_shape=(jax.S...  51.1 us
    unnamed x4, local copies, waits for them, and re-layouts  2.39 us

profile of v3, /device:TPU:1, one launch (start us, length us, event | category | flops | bytes accessed | tf_op | source)
XLA Modules:
  0.0 54.1 jit_solution(13605230634232431896)
XLA Ops:
  0.6 51.1 %elasticity.1 = (f32[1,3,8,32,128]{4,3,2,1,0:T(8,128)}, f32[8,8,32]{2,1,0:T(8,128)}) custom-call(f32[8,8,32]{2,1,0:T(8,128)} %bitcast.3, f32[1,3,8,32,128]{4,3,2,1,0:T(8,128)} %prior_in.1, s32[8,32,128]{2,1,0:T(8,128)} %support_in.1, s32[1,2048]{1,0:T(1,128)} %nodes_in.1, f32[3,1,2048]{2,1,0:T(1,128)} %bitcast.5), custom_call_target="tpu_custom_call" | custom-call | tf_op jit(solution)/shard_map/elasticity/pallas_call | solution.py:985
  51.7 0.0 copy-start
  51.7 1.8 %copy.9 = f32[1,3,8,32,128]{4,3,2,1,0:T(8,128)} copy(f32[1,3,8,32,128]{4,3,2,1,0:T(8,128)} %get-tuple-element.8) | data formatting | bytes 786432
  53.5 0.0 copy-done
  53.5 0.6 %copy.10 = f32[8,32,8]{1,2,0:T(8,128)} copy(f32[8,32,8]{1,2,0:T(8,128)S(1)} %bitcast.4) | data formatting | bytes 16384
Async XLA Ops:
  51.7 1.8 %copy-start = (f32[8,8,32]{2,1,0:T(8,128)S(1)}, f32[8,8,32]{2,1,0:T(8,128)}, u32[]{:S(2)}) copy-start(f32[8,8,32]{2,1,0:T(8,128)} %get-tuple-element.5) | copy-start | bytes 24580

commit v4 on v3

--- a/solution.py
+++ b/solution.py
@@ -27,7 +27,7 @@
 BLOCKS = USED // 8
 CHUNK = 512
 MESH = pl.DeviceIdType.MESH
-AROUND = [(0, -1), (0, 1), (-1, -1), (-1, 1), (1, -1), (1, 1), (-1, 0), (1, 0)]
+AROUND = [(-1, -1), (-1, 1), (1, -1), (1, 1), (0, -1), (0, 1), (-1, 0), (1, 0)]
 
 
 def chebyshev_factors():
@@ -334,6 +334,22 @@
     def toward(dx, dy):
         return (load, gx + dx, gy + dy)
 
+    barrier = pltpu.get_barrier_semaphore()
+    each_peer(
+        lambda step: pl.semaphore_signal(
+            barrier, inc=1, device_id=(peer(step), gx, gy), device_id_type=MESH
+        )
+    )
+    expected = n_load - 1
+    for dx, dy in AROUND:
+        expected = expected + inside(dx, dy).astype(jnp.int32)
+
+        @pl.when(inside(dx, dy))
+        def _():
+            pl.semaphore_signal(
+                barrier, inc=1, device_id=toward(dx, dy), device_id_type=MESH
+            )
+
     fetches = [
         pltpu.make_async_copy(source, target, fetched.at[index])
         for index, (source, target) in enumerate(
@@ -349,55 +365,6 @@
     for fetch in fetches:
         fetch.start()
 
-    for index, (dx, dy) in enumerate(AROUND):
-
-        @pl.when(jnp.logical_not(inside(dx, dy)))
-        def _():
-            if dy == 0:
-                for ref in (beside, beside2):
-                    ref[(dx + 1) // 2] = jnp.zeros(ref.shape[1:], jnp.float32)
-            else:
-                for ref in (packs, packs2):
-                    ref[dx + 1, (dy + 1) // 2] = jnp.zeros(ref.shape[2:], jnp.float32)
-
-    @pl.when(jnp.logical_not(inside(-1, 0)))
-    def _():
-        rows_low[...] = jnp.zeros(rows_low.shape, jnp.float32)
-        fixed_low[...] = jnp.zeros(fixed_low.shape, jnp.int32)
-        corners_low[0] = jnp.zeros(corners_low.shape[1:], jnp.float32)
-        corners_high[0] = jnp.zeros(corners_high.shape[1:], jnp.float32)
-
-    @pl.when(jnp.logical_not(inside(1, 0)))
-    def _():
-        rows_high[...] = jnp.zeros(rows_high.shape, jnp.float32)
-        fixed_high[...] = jnp.zeros(fixed_high.shape, jnp.int32)
-        corners_low[1] = jnp.zeros(corners_low.shape[1:], jnp.float32)
-        corners_high[1] = jnp.zeros(corners_high.shape[1:], jnp.float32)
-
-    @pl.when(jnp.logical_not(inside(0, -1)))
-    def _():
-        columns_low[...] = jnp.zeros(columns_low.shape, jnp.float32)
-
-    @pl.when(jnp.logical_not(inside(0, 1)))
-    def _():
-        columns_high[...] = jnp.zeros(columns_high.shape, jnp.float32)
-
-    barrier = pltpu.get_barrier_semaphore()
-    each_peer(
-        lambda step: pl.semaphore_signal(
-            barrier, inc=1, device_id=(peer(step), gx, gy), device_id_type=MESH
-        )
-    )
-    expected = n_load - 1
-    for dx, dy in AROUND:
-        expected = expected + inside(dx, dy).astype(jnp.int32)
-
-        @pl.when(inside(dx, dy))
-        def _():
-            pl.semaphore_signal(
-                barrier, inc=1, device_id=toward(dx, dy), device_id_type=MESH
-            )
-
     fetches[0].wait()
     for row in range(R):
         raw[row, :, 0:W] = density[row]
@@ -481,25 +448,43 @@
     for dx, copy in row_copies:
         pl.when(inside(dx, 0))(copy.start)
 
+    for index, (dx, dy) in enumerate(AROUND):
+
+        @pl.when(jnp.logical_not(inside(dx, dy)))
+        def _():
+            if dy == 0:
+                for ref in (beside, beside2):
+                    ref[(dx + 1) // 2] = jnp.zeros(ref.shape[1:], jnp.float32)
+            else:
+                for ref in (packs, packs2):
+                    ref[dx + 1, (dy + 1) // 2] = jnp.zeros(ref.shape[2:], jnp.float32)
+
+    @pl.when(jnp.logical_not(inside(-1, 0)))
+    def _():
+        rows_low[...] = jnp.zeros(rows_low.shape, jnp.float32)
+        fixed_low[...] = jnp.zeros(fixed_low.shape, jnp.int32)
+        corners_low[0] = jnp.zeros(corners_low.shape[1:], jnp.float32)
+        corners_high[0] = jnp.zeros(corners_high.shape[1:], jnp.float32)
+
+    @pl.when(jnp.logical_not(inside(1, 0)))
+    def _():
+        rows_high[...] = jnp.zeros(rows_high.shape, jnp.float32)
+        fixed_high[...] = jnp.zeros(fixed_high.shape, jnp.int32)
+        corners_low[1] = jnp.zeros(corners_low.shape[1:], jnp.float32)
+        corners_high[1] = jnp.zeros(corners_high.shape[1:], jnp.float32)
+
+    @pl.when(jnp.logical_not(inside(0, -1)))
+    def _():
+        columns_low[...] = jnp.zeros(columns_low.shape, jnp.float32)
+
+    @pl.when(jnp.logical_not(inside(0, 1)))
+    def _():
+        columns_high[...] = jnp.zeros(columns_high.shape, jnp.float32)
+
+
     def in_grid(row, columns):
         row, columns = row + gx * R, columns + gy * W
         return (row >= 0) & (row < n_x * R) & (columns >= 0) & (columns < n_y * W)
-
-    def set_mask(row, carry):
-        columns = lax.broadcasted_iota(jnp.int32, (48, A), 0) - 8
-        mask[row] = jnp.where(in_grid(row - 8, columns), 1.0, 0.0)
-        return carry
-
-    lax.fori_loop(3, 21, set_mask, 0)
-
-    def set_ring_mask(row, carry):
-        lane = lanes((wide, A))
-        layer = lax.broadcasted_iota(jnp.int32, (wide, A), 0) - 4 + load * depth
-        kept = in_grid(row - 4, lane - 4) & (layer >= 0) & (layer < A) & (lane < W + 8)
-        ring_mask[row] = jnp.where(kept, 1.0, 0.0)
-        return carry
-
-    lax.fori_loop(1, 15, set_ring_mask, 0)
 
     def halo_copy(step, part):
         span = pl.ds(part * 3 * A, 3 * A)
@@ -559,7 +544,8 @@
             )
         return carry
 
-    lax.fori_loop(0, load_nodes.shape[1] // CHUNK, add_loads, 0)
+    chunks = load_nodes.shape[1] // CHUNK
+    lax.fori_loop(0, chunks // 2, add_loads, 0)
 
     for index, (dx, dy) in enumerate(AROUND):
         if dy != 0:
@@ -598,21 +584,23 @@
     for dx, copy in corner_copies:
         pl.when(inside(dx, 0))(copy.start)
 
-    for ref in waves[:4] + ring_waves[:4]:
-
-        def clear(row, carry):
-            ref[row] = jnp.zeros(ref.shape[1:], jnp.float32)
-            return carry
-
-        lax.fori_loop(0, ref.shape[0], clear, 0)
-
-    def clear_rows(row, carry):
-        for c in range(3):
-            field[c, row, W:PITCH, :] = jnp.zeros((PITCH - W, A), jnp.float32)
-        free[row] = jnp.zeros((PITCH, A), jnp.float32)
+    lax.fori_loop(chunks // 2, chunks, add_loads, 0)
+
+    def set_mask(row, carry):
+        columns = lax.broadcasted_iota(jnp.int32, (48, A), 0) - 8
+        mask[row] = jnp.where(in_grid(row - 8, columns), 1.0, 0.0)
         return carry
 
-    lax.fori_loop(0, ROWS, clear_rows, 0)
+    in_groups(3, 21, 3, set_mask)
+
+    def set_ring_mask(row, carry):
+        lane = lanes((wide, A))
+        layer = lax.broadcasted_iota(jnp.int32, (wide, A), 0) - 4 + load * depth
+        kept = in_grid(row - 4, lane - 4) & (layer >= 0) & (layer < A) & (lane < W + 8)
+        ring_mask[row] = jnp.where(kept, 1.0, 0.0)
+        return carry
+
+    in_groups(1, 15, 7, set_ring_mask)
 
     for c in range(3):
         for row in range(R):
@@ -660,14 +648,14 @@
         free[row] = jnp.where(kept & (free[row] == 0.0), 1.0, 0.0)
         return carry
 
-    lax.fori_loop(1, 12, set_free, 0)
+    in_groups(1, 12, 4, set_free)
 
     def lift(row, carry):
         for c in range(3):
             lifted[c, row] = lane_up(field[c, row])
         return carry
 
-    lax.fori_loop(0, ROWS, lift, 0)
+    in_groups(0, ROWS, 4, lift)
 
     def place(block, pieces):
         value = block.T
@@ -819,29 +807,29 @@
     energy[0:4, :] = jnp.zeros((4, 2 * A), jnp.float32)
     energy[4 + A : 8 + A, :] = jnp.zeros((4, 2 * A), jnp.float32)
 
-    for c in range(3):
-        for row in range(R):
-            prior[0, c, row] = field[c, row + 2, 2 : 2 + W, :]
-    leave = pltpu.make_async_copy(prior, displacement, fetched.at[5])
-    leave.start()
-
     def slab(owner):
         return pl.ds(pl.multiple_of(owner * depth, 8), wide)
 
     def share_copy(step):
         return remote(
             energy.at[slab(peer(step)), :],
-            shares.at[load],
+            shares.at[step],
             share_send.at[step],
             share_recv.at[step],
             (peer(step), gx, gy),
         )
 
     each_peer(lambda step: share_copy(step).start())
-    shares[load] = energy[slab(load), :]
+    for c in range(3):
+        for row in range(R):
+            displacement[0, c, row] = field[c, row + 2, 2 : 2 + W, :]
+
+    scale = -(2.0 / n_load) * weights[slab(load), :]
     each_peer(lambda step: share_copy(step).wait_recv())
-    summed = total([shares[index] for index in range(n_load)])
-    value = -(2.0 / n_load) * weights[slab(load), :] * summed
+    value = energy[slab(load), :]
+    for step in range(n_load - 1):
+        value = value + shares[step]
+    value = scale * value
     share[...] = value
     share_pack[...] = fold_pack([value[:, 0:A], value[:, A : 2 * A]])
 
@@ -900,7 +888,6 @@
         summed = total([ref[row + 4, 12 : 12 + depth, :] for ref in ring_waves])
         sensitivity[row] = turned(summed, -4)[:, 0:W]
 
-    leave.wait()
     for index, (dx, dy) in enumerate(AROUND):
 
         @pl.when(inside(dx, dy))
@@ -981,19 +968,19 @@
         ((24, 48, A), real),
         ((16, wide, A), real),
     ]
-    semaphores = [8, 8, n_load, n_load, (2, n_load), (2, n_load), 4, 4, 2, 2, 4, 4, n_load, n_load, 8, 8, 6]
+    semaphores = [8, 8, n_load, n_load, (2, n_load), (2, n_load), 4, 4, 2, 2, 4, 4, n_load, n_load, 8, 8, 5]
     displacement, sensitivity = pl.pallas_call(
         functools.partial(kernel, counts, depth),
         out_shape=(
-            jax.ShapeDtypeStruct(displacement_prior.shape, real),
-            jax.ShapeDtypeStruct((R, depth, W), real),
+            pltpu.VMEM(displacement_prior.shape, real),
+            pltpu.VMEM((R, depth, W), real),
         ),
         in_specs=[pl.BlockSpec(memory_space=pltpu.HBM)] * 5,
-        out_specs=(pl.BlockSpec(memory_space=pltpu.HBM), pl.BlockSpec(memory_space=pltpu.VMEM)),
+        out_specs=(pl.BlockSpec(memory_space=pltpu.VMEM),) * 2,
         scratch_shapes=[pltpu.VMEM(shape, kind) for shape, kind in scratch]
         + [pltpu.SemaphoreType.DMA(count if isinstance(count, tuple) else (count,)) for count in semaphores],
         compiler_params=pltpu.CompilerParams(
-            collective_id=0, has_side_effects=True, vmem_limit_bytes=67_043_328
+            collective_id=0, has_side_effects=True, vmem_limit_bytes=67_043_328 - (1 << 19),
         ),
         name="elasticity",
     )(

time: 54.3 us -> 51 us (0.939)
  Pallas kernels: 51.1 us -> 48.9 us
  local copies, waits for them, and re-layouts: 2.39 us -> 1.36 us
    pallas_call x1, Pallas kernels: 51.1 us -> 48.9 us  [body(): pl.pallas_call(functools.partial(kernel, counts, depth), out_shape=(pltpu...]
    unnamed x4 -> x2, local copies, waits for them, and re-layouts: 2.39 us -> 1.36 us
where the time goes in v4:
time: 51 us; the launch traced here: 50.9 us
  Pallas kernels  48.9 us (96%)
  local copies, waits for them, and re-layouts  1.36 us (3%)
  between operations  0.64 us (1%)
    pallas_call x1, Pallas kernels, body(): pl.pallas_call(functools.partial(kernel, counts, depth), out_shape=(pltpu...  48.9 us
    unnamed x2, local copies, waits for them, and re-layouts  1.36 us

profile of v4, /device:TPU:1, one launch (start us, length us, event | category | flops | bytes accessed | tf_op | source)
XLA Modules:
  0.0 50.9 jit_solution(8779822665962849050)
XLA Ops:
  0.6 48.9 %elasticity.1 = (f32[1,3,8,32,128]{4,3,2,1,0:T(8,128)S(1)}, f32[8,8,32]{2,1,0:T(8,128)S(1)}) custom-call(f32[8,8,32]{2,1,0:T(8,128)} %bitcast.4, f32[1,3,8,32,128]{4,3,2,1,0:T(8,128)} %prior_in.1, s32[8,32,128]{2,1,0:T(8,128)} %support_in.1, s32[1,2048]{1,0:T(1,128)} %nodes_in.1, f32[3,1,2048]{2,1,0:T(1,128)} %bitcast.5), custom_call_target="tpu_custom_call" | custom-call | tf_op jit(solution)/shard_map/elasticity/pallas_call | solution.py:972
  49.5 0.7 %copy.9 = f32[1,3,8,32,128]{4,3,2,1,0:T(8,128)} copy(f32[1,3,8,32,128]{4,3,2,1,0:T(8,128)S(1)} %get-tuple-element.6) | data formatting | bytes 786432
  50.3 0.6 %copy.10 = f32[8,32,8]{1,2,0:T(8,128)} copy(f32[8,32,8]{1,2,0:T(8,128)S(1)} %bitcast.3) | data formatting | bytes 16384

commit v5 on v4

--- a/solution.py
+++ b/solution.py
@@ -682,7 +682,7 @@
         wave[row, 8:56, :] = wave[row, 8:56, :] / theta
         return carry
 
-    in_groups(2, 22, 5, start_filter)
+    in_groups(2, 22, 20, start_filter)
     for sweep, (own_factor, last_factor, near_factor) in enumerate(terms):
 
         def one_row(row, carry, source=waves[sweep], target=waves[sweep + 1]):
@@ -701,7 +701,7 @@
             target[row, 8:56, :] = direction * mask[row]
             return carry
 
-        in_groups(3 + sweep, 21 - sweep, 3, one_row)
+        in_groups(3 + sweep, 21 - sweep, 18, one_row)
 
     def set_modulus(row, carry):
         filtered = total([ref[row + 6, 14 : 14 + USED, :] for ref in waves])
@@ -713,7 +713,7 @@
         )
         return carry
 
-    in_groups(0, 12, 3, set_modulus)
+    in_groups(0, 12, 12, set_modulus)
     for half in range(2):
         tall = result[2 + 4 * half : 6 + 4 * half, 2 : 2 + W, :].reshape(A, A)
         weights[4 : 4 + A, A * half : A * half + A] = tall.T
@@ -728,7 +728,7 @@
         step_size[row] = relax_factor / ((lame + 4 * shear) / 9 * around_node)
         return carry
 
-    in_groups(1, 12, 4, set_step)
+    in_groups(1, 12, 11, set_step)
 
     for sweep in range(JACOBI):
         first, last = 1 + sweep, 12 - sweep
@@ -770,7 +770,7 @@
             in_groups(
                 first - 1,
                 last,
-                (last - first + 1) // 2,
+                last - first + 1,
                 one_element_row,
                 ([low[key] for key in KEYS], nothing),
             )
@@ -789,7 +789,7 @@
                 lifted[c, row, span, :] = lane_up(moved)
             return carry
 
-        in_groups(first, last, 2, one_node_row)
+        in_groups(first, last, 4, one_node_row)
 
     for block in range(W // 8):
 
@@ -800,7 +800,7 @@
             return [high[key] for key in KEYS]
 
         low = plane_sums(field, lifted, 2, 8 * block + 2)
-        in_groups(2, 10, 4, one_energy_row, [low[key] for key in KEYS])
+        in_groups(2, 10, 8, one_energy_row, [low[key] for key in KEYS])
     for half in range(2):
         tall = remain[2 + 4 * half : 6 + 4 * half, 0:W, :].reshape(A, A)
         energy[4 : 4 + A, A * half : A * half + A] = tall.T

time: 51 us -> 48.4 us (0.949)
  Pallas kernels: 48.9 us -> 46.2 us
    pallas_call x1, Pallas kernels: 48.9 us -> 46.2 us  [body(): pl.pallas_call(functools.partial(kernel, counts, depth), out_shape=(pltpu...]
where the time goes in v5:
time: 48.4 us; the launch traced here: 48.3 us
  Pallas kernels  46.2 us (95%)
  local copies, waits for them, and re-layouts  1.36 us (3%)
  between operations  0.64 us (1%)
    pallas_call x1, Pallas kernels, body(): pl.pallas_call(functools.partial(kernel, counts, depth), out_shape=(pltpu...  46.2 us
    unnamed x2, local copies, waits for them, and re-layouts  1.36 us

profile of v5, /device:TPU:1, one launch (start us, length us, event | category | flops | bytes accessed | tf_op | source)
XLA Modules:
  0.0 48.3 jit_solution(17286641049736966390)
XLA Ops:
  0.6 46.2 %elasticity.1 = (f32[1,3,8,32,128]{4,3,2,1,0:T(8,128)S(1)}, f32[8,8,32]{2,1,0:T(8,128)S(1)}) custom-call(f32[8,8,32]{2,1,0:T(8,128)} %bitcast.4, f32[1,3,8,32,128]{4,3,2,1,0:T(8,128)} %prior_in.1, s32[8,32,128]{2,1,0:T(8,128)} %support_in.1, s32[1,2048]{1,0:T(1,128)} %nodes_in.1, f32[3,1,2048]{2,1,0:T(1,128)} %bitcast.5), custom_call_target="tpu_custom_call" | custom-call | tf_op jit(solution)/shard_map/elasticity/pallas_call | solution.py:972
  46.9 0.7 %copy.9 = f32[1,3,8,32,128]{4,3,2,1,0:T(8,128)} copy(f32[1,3,8,32,128]{4,3,2,1,0:T(8,128)S(1)} %get-tuple-element.6) | data formatting | bytes 786432
  47.6 0.6 %copy.10 = f32[8,32,8]{1,2,0:T(8,128)} copy(f32[8,32,8]{1,2,0:T(8,128)S(1)} %bitcast.3) | data formatting | bytes 16384
